TPU v7x, 32 devices: a whole 2x2x4 slice. The times are simulated.
32 devices in a mesh: rep: 8 (over y, x, core), fsdp: 4 (over z).
Axes of the slice: x: 2, y: 2, z: 4, core: 2. Of those that a mesh axis runs over, the one named last changes fastest.
Arguments:
- tokens: bfloat16 [16384, 960], P(('rep', 'fsdp')), may hold values from -6 to 6
- sequence_ids: int32 [16384], P(('rep', 'fsdp')), may hold values from 0 to 7, as said below
- cotangent: bfloat16 [16384, 960], P(('rep', 'fsdp')), may hold values from -6 to 6
- norm_gains: float32 [2, 960], P(None, 'fsdp'), may hold values from 0.5 to 1.5
- qkv_weight: float32 [960, 1600], P('fsdp'), as said below
- out_weight: float32 [960, 960], P('fsdp'), may hold values from -0.5 to 0.5
- gate_up_weight: float32 [960, 5120], P('fsdp'), may hold values from -0.1875 to 0.1875
- down_weight: float32 [2560, 960], P('fsdp'), may hold values from -0.125 to 0.125
- gains_first: float32 [2, 960], P(None, 'fsdp'), may hold values from -40 to 40
- qkv_first: float32 [960, 1600], P('fsdp'), may hold values from -40 to 40
- out_first: float32 [960, 960], P('fsdp'), may hold values from -40 to 40
- gate_up_first: float32 [960, 5120], P('fsdp'), may hold values from -40 to 40
- down_first: float32 [2560, 960], P('fsdp'), may hold values from -40 to 40
- gains_second: float32 [2, 960], P(None, 'fsdp'), may hold values from 32.768 to 491.52
- qkv_second: float32 [960, 1600], P('fsdp'), may hold values from 32.768 to 491.52
- out_second: float32 [960, 960], P('fsdp'), may hold values from 32.768 to 491.52
- gate_up_second: float32 [960, 5120], P('fsdp'), may hold values from 32.768 to 491.52
- down_second: float32 [2560, 960], P('fsdp'), may hold values from 32.768 to 491.52
Outputs:
- block_out: bfloat16 [16384, 960], P(('rep', 'fsdp'))
- tokens_grad: bfloat16 [16384, 960], P(('rep', 'fsdp'))
- gains_grad: float32 [2, 960], P(None, 'fsdp')
- qkv_grad: float32 [960, 1600], P('fsdp')
- out_grad: float32 [960, 960], P('fsdp')
- gate_up_grad: float32 [960, 5120], P('fsdp')
- down_grad: float32 [2560, 960], P('fsdp')
- gains_delta: float32 [2, 960], P(None, 'fsdp')
- qkv_delta: float32 [960, 1600], P('fsdp')
- out_delta: float32 [960, 960], P('fsdp')
- gate_up_delta: float32 [960, 5120], P('fsdp')
- down_delta: float32 [2560, 960], P('fsdp')
- gains_first_new: float32 [2, 960], P(None, 'fsdp')
- qkv_first_new: float32 [960, 1600], P('fsdp')
- out_first_new: float32 [960, 960], P('fsdp')
- gate_up_first_new: float32 [960, 5120], P('fsdp')
- down_first_new: float32 [2560, 960], P('fsdp')
- gains_second_new: float32 [2, 960], P(None, 'fsdp')
- qkv_second_new: float32 [960, 1600], P('fsdp')
- out_second_new: float32 [960, 960], P('fsdp')
- gate_up_second_new: float32 [960, 5120], P('fsdp')
- down_second_new: float32 [2560, 960], P('fsdp')
Inputs may be any that keep to these rules, and one draw needn't show every extreme that they name: `sequence_ids`: along each device's 512 tokens the numbers start at 0 and never fall; some device holds a single sequence of 512 tokens, and some device holds 8 sequences of 64 tokens each. `qkv_weight`: float32 weights.
All inputs are finite; a program needn't handle non-finite values.
Results may differ from a plain program's by a relative error of at most 0.022.
The roundings to bfloat16 on the way count: a program that leaves them out, or rounds other values in their place, can miss the bound.
Values may be sent and summed in bfloat16 or wider, within the bound.
A program may use at most 256 MiB of HBM per device.

v0:
```python
import math

import jax
import jax.numpy as jnp
from jax import lax
from jax.experimental import pallas as pl
from jax.experimental.pallas import tpu as pltpu
from jax.sharding import PartitionSpec as P
D = 960
HEADS = 15
KV_HEADS = 5
HEAD = 64
FF = 2560
STEP = 4


NORM_EPS = 1e-05
ROPE_BASE = 100000.0
LEARN_RATE = 0.03
BETA_ONE = 0.9
BETA_TWO = 0.95
ADAM_EPS = 1e-08
DECAY_RATE = 0.1
NEG_LARGE = -1e30


def positions(sequence_ids):
    row_index = jnp.arange(sequence_ids.shape[0], dtype=jnp.int32)
    prior_ids = jnp.concatenate([jnp.full((1,), -1, jnp.int32), sequence_ids[:-1]])
    seq_starts = jnp.where(sequence_ids != prior_ids, row_index, 0)
    first_row = lax.cummax(seq_starts, axis=0)
    return (row_index - first_row).astype(jnp.float32)


def causal_mask(sequence_ids):
    row_index = jnp.arange(sequence_ids.shape[0], dtype=jnp.int32)
    return (sequence_ids[:, None] == sequence_ids[None, :]) & (
        row_index[None, :] <= row_index[:, None]
    )


def rope_tables(places):
    half_size = HEAD // 2
    freq_table = ROPE_BASE ** (-2.0 * jnp.arange(half_size, dtype=jnp.float32) / HEAD)
    angles = places[:, None] * freq_table[None, :]
    return (jnp.cos(angles), jnp.sin(angles))


def rotate(vectors, cosine_table, sine_table):
    half_size = vectors.shape[-1] // 2
    first_half = vectors[..., :half_size]
    second_half = vectors[..., half_size:]
    cosine_wide = cosine_table[:, None, :]
    sine_wide = sine_table[:, None, :]
    return jnp.concatenate(
        [
            first_half * cosine_wide - second_half * sine_wide,
            second_half * cosine_wide + first_half * sine_wide,
        ],
        axis=-1,
    )


def rms_norm(values, gain_row):
    row_scale = lax.rsqrt(jnp.mean(values * values, axis=-1, keepdims=True) + NORM_EPS)
    return values * row_scale * gain_row


def swiglu(gate_part, up_part):
    return gate_part * jax.nn.sigmoid(gate_part) * up_part


def adamw_update(weight, moment_one, moment_two, gradient, decay_rate):
    first_new = BETA_ONE * moment_one + (1.0 - BETA_ONE) * gradient
    second_new = BETA_TWO * moment_two + (1.0 - BETA_TWO) * gradient * gradient
    fix_one = 1.0 - BETA_ONE**STEP
    fix_two = 1.0 - BETA_TWO**STEP
    update_dir = (
        first_new / fix_one / (jnp.sqrt(second_new / fix_two) + ADAM_EPS) + decay_rate * weight
    )
    return (-LEARN_RATE * update_dir, first_new, second_new)


def split_groups(queries, keys_rot, values_kv):
    count_rows = queries.shape[0]
    group_size = HEADS // KV_HEADS
    query_groups = queries.reshape(count_rows, KV_HEADS, group_size, HEAD).transpose(1, 2, 0, 3)
    return (query_groups, keys_rot.transpose(1, 0, 2), values_kv.transpose(1, 0, 2))


def attend(queries, keys_rot, values_kv, mask_table):
    count_rows = queries.shape[0]
    scale_factor = 1.0 / math.sqrt(HEAD)
    query_groups, key_groups, value_groups = split_groups(queries, keys_rot, values_kv)

    def one_group(members):
        query_one, key_one, value_one = members
        scores = (
            jnp.einsum("gqd,kd->gqk", query_one, key_one, preferred_element_type=jnp.float32)
            * scale_factor
        )
        scores = jnp.where(mask_table[None], scores, NEG_LARGE)
        top_score = jnp.max(scores, axis=-1, keepdims=True)
        weights = jnp.exp(scores - top_score)
        total_sum = jnp.sum(weights, axis=-1, keepdims=True)
        prob_table = (weights / total_sum).astype(jnp.bfloat16)
        context_one = jnp.einsum(
            "gqk,kd->gqd", prob_table, value_one, preferred_element_type=jnp.float32
        )
        return (context_one.astype(jnp.bfloat16), (top_score + jnp.log(total_sum))[..., 0])

    context_groups, log_total = lax.map(one_group, (query_groups, key_groups, value_groups))
    context = context_groups.transpose(2, 0, 1, 3).reshape(count_rows, HEADS, HEAD)
    return (context, log_total)


def attend_back(queries, keys_rot, values_kv, mask_table, log_total, grad_context):
    count_rows = queries.shape[0]
    group_size = HEADS // KV_HEADS
    scale_factor = 1.0 / math.sqrt(HEAD)
    query_groups, key_groups, value_groups = split_groups(queries, keys_rot, values_kv)
    grad_groups = grad_context.reshape(count_rows, KV_HEADS, group_size, HEAD).transpose(1, 2, 0, 3)

    def one_group(members):
        query_one, key_one, value_one, log_one, grad_one = members
        scores = (
            jnp.einsum("gqd,kd->gqk", query_one, key_one, preferred_element_type=jnp.float32)
            * scale_factor
        )
        scores = jnp.where(mask_table[None], scores, NEG_LARGE)
        prob_table = jnp.exp(scores - log_one[..., None])
        grad_probs = jnp.einsum(
            "gqd,kd->gqk", grad_one, value_one, preferred_element_type=jnp.float32
        )
        grad_value = jnp.einsum(
            "gqk,gqd->kd",
            prob_table.astype(jnp.bfloat16),
            grad_one,
            preferred_element_type=jnp.float32,
        )
        row_delta = jnp.sum(prob_table * grad_probs, axis=-1, keepdims=True)
        grad_scores = (prob_table * (grad_probs - row_delta)).astype(jnp.bfloat16)
        grad_query = (
            jnp.einsum("gqk,kd->gqd", grad_scores, key_one, preferred_element_type=jnp.float32)
            * scale_factor
        )
        grad_key = (
            jnp.einsum("gqk,gqd->kd", grad_scores, query_one, preferred_element_type=jnp.float32)
            * scale_factor
        )
        return (grad_query, grad_key, grad_value)

    grad_q_groups, grad_k_groups, grad_v_groups = lax.map(
        one_group, (query_groups, key_groups, value_groups, log_total, grad_groups)
    )
    grad_queries = grad_q_groups.transpose(2, 0, 1, 3).reshape(count_rows, HEADS, HEAD)
    return (grad_queries, grad_k_groups.transpose(1, 0, 2), grad_v_groups.transpose(1, 0, 2))


def forward(tokens, sequence_ids, attn_set, mlp_set):
    gain_half, qkv_half, out_half = attn_set
    gate_up_half, down_half = mlp_set
    count_rows = tokens.shape[0]
    kv_width = KV_HEADS * HEAD
    inputs = tokens.astype(jnp.float32)
    gain_rows = gain_half.astype(jnp.float32)
    normed = rms_norm(inputs, gain_rows[0]).astype(jnp.bfloat16)
    mixed_cols = jnp.dot(normed, qkv_half, preferred_element_type=jnp.float32)
    cosine_table, sine_table = rope_tables(positions(sequence_ids))
    queries = rotate(
        mixed_cols[:, :D].reshape(count_rows, HEADS, HEAD), cosine_table, sine_table
    ).astype(jnp.bfloat16)
    keys_rot = rotate(
        mixed_cols[:, D : D + kv_width].reshape(count_rows, KV_HEADS, HEAD),
        cosine_table,
        sine_table,
    ).astype(jnp.bfloat16)
    values_kv = (
        mixed_cols[:, D + kv_width :].reshape(count_rows, KV_HEADS, HEAD).astype(jnp.bfloat16)
    )
    context, log_total = attend(queries, keys_rot, values_kv, causal_mask(sequence_ids))
    middle = inputs + jnp.dot(
        context.reshape(count_rows, D), out_half, preferred_element_type=jnp.float32
    )
    normed_two = rms_norm(middle, gain_rows[1]).astype(jnp.bfloat16)
    gate_up = jnp.dot(normed_two, gate_up_half, preferred_element_type=jnp.float32)
    hidden = swiglu(gate_up[:, :FF], gate_up[:, FF:]).astype(jnp.bfloat16)
    result = middle + jnp.dot(hidden, down_half, preferred_element_type=jnp.float32)
    kept_state = (
        inputs,
        normed,
        queries,
        keys_rot,
        values_kv,
        context,
        log_total,
        middle,
        normed_two,
        gate_up,
        hidden,
    )
    return (kept_state, result)


def mlp_backward(kept_state, cotangent, attn_set, mlp_set):
    middle, normed_two, gate_up, hidden = (
        kept_state[7],
        kept_state[8],
        kept_state[9],
        kept_state[10],
    )
    gain_rows = attn_set[0].astype(jnp.float32)
    gate_up_half, down_half = mlp_set
    grad_result = cotangent.astype(jnp.float32)
    grad_branch = grad_result.astype(jnp.bfloat16)
    down_grad = jnp.einsum("rf,rd->fd", hidden, grad_branch, preferred_element_type=jnp.float32)
    grad_hidden = jnp.einsum(
        "rd,fd->rf", grad_branch, down_half, preferred_element_type=jnp.float32
    )
    _, act_back = jax.vjp(swiglu, gate_up[:, :FF], gate_up[:, FF:])
    grad_gate, grad_up = act_back(grad_hidden)
    grad_mix_two = jnp.concatenate([grad_gate, grad_up], axis=1).astype(jnp.bfloat16)
    gate_up_grad = jnp.einsum(
        "rd,rf->df", normed_two, grad_mix_two, preferred_element_type=jnp.float32
    )
    grad_normed_two = jnp.einsum(
        "rf,df->rd", grad_mix_two, gate_up_half, preferred_element_type=jnp.float32
    )
    _, norm_back_two = jax.vjp(rms_norm, middle, gain_rows[1])
    grad_middle_norm, gain_two_grad = norm_back_two(grad_normed_two)
    grad_middle = grad_result + grad_middle_norm
    return ((gate_up_grad, down_grad), (grad_middle, gain_two_grad))


def attn_backward(kept_state, carried, sequence_ids, attn_set):
    inputs, normed, queries, keys_rot, values_kv, context, log_total = kept_state[:7]
    grad_middle, gain_two_grad = carried
    gain_half, qkv_half, out_half = attn_set
    gain_rows = gain_half.astype(jnp.float32)
    count_rows = inputs.shape[0]
    kv_width = KV_HEADS * HEAD
    grad_attn = grad_middle.astype(jnp.bfloat16)
    flat_context = context.reshape(count_rows, D)
    out_grad = jnp.einsum("rc,rd->cd", flat_context, grad_attn, preferred_element_type=jnp.float32)
    grad_context = jnp.einsum("rd,cd->rc", grad_attn, out_half, preferred_element_type=jnp.float32)
    grad_context = grad_context.astype(jnp.bfloat16).reshape(count_rows, HEADS, HEAD)
    grad_queries, grad_keys, grad_values = attend_back(
        queries, keys_rot, values_kv, causal_mask(sequence_ids), log_total, grad_context
    )
    cosine_table, sine_table = rope_tables(positions(sequence_ids))
    grad_q_raw = rotate(grad_queries, cosine_table, -sine_table).reshape(count_rows, D)
    grad_k_raw = rotate(grad_keys, cosine_table, -sine_table).reshape(count_rows, kv_width)
    grad_mixed = jnp.concatenate(
        [grad_q_raw, grad_k_raw, grad_values.reshape(count_rows, kv_width)], axis=1
    )
    grad_mixed = grad_mixed.astype(jnp.bfloat16)
    qkv_grad = jnp.einsum("rd,rc->dc", normed, grad_mixed, preferred_element_type=jnp.float32)
    grad_normed = jnp.einsum("rc,dc->rd", grad_mixed, qkv_half, preferred_element_type=jnp.float32)
    _, norm_back_one = jax.vjp(rms_norm, inputs, gain_rows[0])
    grad_inputs_norm, gain_one_grad = norm_back_one(grad_normed)
    tokens_grad = (grad_middle + grad_inputs_norm).astype(jnp.bfloat16)
    gains_grad = jnp.stack([gain_one_grad, gain_two_grad])
    return (tokens_grad, (gains_grad, qkv_grad, out_grad))


def on_device_any(
    tokens,
    sequence_ids,
    cotangent,
    norm_gains,
    qkv_weight,
    out_weight,
    gate_up_weight,
    down_weight,
    gains_first,
    qkv_first,
    out_first,
    gate_up_first,
    down_first,
    gains_second,
    qkv_second,
    out_second,
    gate_up_second,
    down_second,
):
    shares = lax.axis_size("rep")
    share = lax.axis_index("rep")
    both = ("fsdp", "rep")
    group = lax.axis_size("fsdp")

    def collect(shard):
        flat = shard.astype(jnp.bfloat16).reshape(shares, -1)
        piece = lax.dynamic_index_in_dim(flat, share, 0, keepdims=False)
        whole = lax.all_gather(piece, both, axis=0, tiled=True)
        return whole.reshape(shard.shape[0] * group, shard.shape[1])

    def total(gradient, shard):
        piece = lax.psum_scatter(
            gradient.astype(jnp.bfloat16).reshape(-1), both, scatter_dimension=0, tiled=True
        )
        flat = lax.all_gather(piece, "rep", axis=0, tiled=True)
        return flat.reshape(shard.shape).astype(jnp.float32)

    gain_full = lax.all_gather(norm_gains.astype(jnp.bfloat16), "fsdp", axis=1, tiled=True)
    qkv_full = collect(qkv_weight)
    out_full = collect(out_weight)
    mlp_set = (collect(gate_up_weight), collect(down_weight))
    attn_set = (gain_full, qkv_full, out_full)
    kept_state, result = forward(tokens, sequence_ids, attn_set, mlp_set)
    block_out = result.astype(jnp.bfloat16)
    mlp_grads, carried = mlp_backward(kept_state, cotangent, attn_set, mlp_set)
    down_total = total(mlp_grads[1], down_weight)
    gate_up_total = total(mlp_grads[0], gate_up_weight)
    tokens_grad, attn_grads = attn_backward(kept_state, carried, sequence_ids, attn_set)
    gains_part = lax.psum_scatter(attn_grads[0], "fsdp", scatter_dimension=1, tiled=True)
    gains_total = lax.psum(gains_part, "rep")
    qkv_total = total(attn_grads[1], qkv_weight)
    out_total = total(attn_grads[2], out_weight)
    gains_delta, gains_first_new, gains_second_new = adamw_update(
        norm_gains, gains_first, gains_second, gains_total, 0.0
    )
    qkv_delta, qkv_first_new, qkv_second_new = adamw_update(
        qkv_weight, qkv_first, qkv_second, qkv_total, DECAY_RATE
    )
    out_delta, out_first_new, out_second_new = adamw_update(
        out_weight, out_first, out_second, out_total, DECAY_RATE
    )
    gate_up_delta, gate_up_first_new, gate_up_second_new = adamw_update(
        gate_up_weight, gate_up_first, gate_up_second, gate_up_total, DECAY_RATE
    )
    down_delta, down_first_new, down_second_new = adamw_update(
        down_weight, down_first, down_second, down_total, DECAY_RATE
    )
    return (
        block_out,
        tokens_grad,
        gains_total,
        qkv_total,
        out_total,
        gate_up_total,
        down_total,
        gains_delta,
        qkv_delta,
        out_delta,
        gate_up_delta,
        down_delta,
        gains_first_new,
        qkv_first_new,
        out_first_new,
        gate_up_first_new,
        down_first_new,
        gains_second_new,
        qkv_second_new,
        out_second_new,
        gate_up_second_new,
        down_second_new,
    )


MESH = pl.DeviceIdType.MESH
bf16, f32 = jnp.bfloat16, jnp.float32
ROWS = 2560
GATHER_UNITS = [(0, 240, 128), (240, 240, 128), (480, 240, 128)] + [(720 + 368 * j, 368, 192) for j in range(5)]
REDUCE_UNITS = [(720 + 368 * j, 368, 192) for j in range(5)] + [(480, 240, 128), (0, 240, 128), (240, 240, 128)]
NT = (((1,), (1,)), ((), ()))
NN = (((1,), (0,)), ((), ()))
TN = (((0,), (0,)), ((), ()))


def mm(a, b, dims=NN):
    return lax.dot_general(a, b, dims, preferred_element_type=f32)


def lanes(n=128):
    return lax.broadcasted_iota(jnp.int32, (1, n), 1)


def spread(k):
    return jnp.where(k < 3, k, k - 1)


def param_specs():
    return [
        pl.BlockSpec((2, 240), lambda k: (0, 0)),
        pl.BlockSpec((240, 256), lambda k: (0, spread(k))),
        pl.BlockSpec((240, 128), lambda k: (0, k)),
        pl.BlockSpec((240, 640), lambda k: (0, k)),
        pl.BlockSpec((128, 640), lambda k: (k, 0)),
    ]


def pack_kernel(gains, qkv, out, gu, dnT, own):
    k = pl.program_id(0)
    own[0, 0:240] = qkv[:, 0:128].astype(bf16)
    own[0, 240:480] = qkv[:, 128:256].astype(bf16)

    @pl.when(k % 4 == 3)
    def _():
        row = jnp.where(k == 3, gains[0:1], gains[1:2])
        tile = jnp.where(lax.broadcasted_iota(jnp.int32, (128, 240), 0) == 0, row, 0.0)
        own[0, 240:480] = jnp.swapaxes(tile, 0, 1).astype(bf16)

    own[0, 480:720] = jnp.where(lanes() < 960 - k * 128, out[...], 0.0).astype(bf16)
    for j in range(5):
        own[0, 720 + 368 * j : 960 + 368 * j] = gu[:, j * 128 : (j + 1) * 128].astype(bf16)
        t = jnp.swapaxes(dnT[:, j * 128 : (j + 1) * 128], 0, 1)
        own[0, 960 + 368 * j : 1088 + 368 * j] = jnp.where(lanes() < 960 - k * 128, t, 0.0).astype(bf16)


def pack(norm_gains, qkv, out, gu, down):
    return pl.pallas_call(
        pack_kernel,
        name="pack",
        grid=(8,),
        out_shape=jax.ShapeDtypeStruct((8, ROWS, 128), bf16),
        in_specs=param_specs(),
        out_specs=pl.BlockSpec((1, ROWS, 128), lambda k: (k, 0, 0)),
    )(norm_gains, qkv, out, gu, down.T)


def adam_kernel(FIN, *refs):
    weight, first, second = refs[0:5], refs[5:10], refs[10:15]
    grad, delta, first_new, second_new = refs[15:20], refs[20:25], refs[25:30], refs[30:35]
    k = pl.program_id(0)
    every = slice(None)

    def update(i, at, g, rate):
        m = BETA_ONE * first[i][at] + (1.0 - BETA_ONE) * g
        v = BETA_TWO * second[i][at] + (1.0 - BETA_TWO) * g * g
        step = m * (1.0 / (1.0 - BETA_ONE**STEP)) / (jnp.sqrt(v * (1.0 / (1.0 - BETA_TWO**STEP))) + ADAM_EPS)
        if rate:
            step = step + rate * weight[i][at]
        grad[i][at] = g
        delta[i][at] = -LEARN_RATE * step
        first_new[i][at] = m
        second_new[i][at] = v

    def rows(a, b):
        return FIN[0, a:b].astype(f32)

    @pl.when(k != 3)
    def _():
        update(1, (every, slice(0, 128)), rows(0, 240), DECAY_RATE)
        update(1, (every, slice(128, 256)), rows(240, 480), DECAY_RATE)

    for i in range(2):

        @pl.when(k == 3 + 4 * i)
        def _():
            update(0, (slice(i, i + 1), every), jnp.swapaxes(rows(240, 480), 0, 1)[0:1], 0.0)

    update(2, (every, every), rows(480, 720), DECAY_RATE)
    for j in range(5):
        c = slice(j * 128, (j + 1) * 128)
        update(3, (every, c), rows(720 + 368 * j, 960 + 368 * j), DECAY_RATE)
        update(4, (every, c), jnp.swapaxes(rows(960 + 368 * j, 1088 + 368 * j), 0, 1), DECAY_RATE)


def adam(FIN, weights, moments):
    def five(group):
        return [*group[:4], group[4].T]

    ins = five(weights) + five(moments[:5]) + five(moments[5:])
    shapes = [jax.ShapeDtypeStruct(a.shape, f32) for a in ins[:5]] * 4
    outs = pl.pallas_call(
        adam_kernel,
        name="adam",
        grid=(8,),
        out_shape=shapes,
        in_specs=[pl.BlockSpec((1, ROWS, 128), lambda k: (k, 0, 0))] + param_specs() * 3,
        out_specs=param_specs() * 4,
    )(FIN, *ins)
    return [o.T if i % 5 == 4 else o for i, o in enumerate(outs)]


class Where:
    def __init__(w):
        rep, z = lax.axis_index("rep"), lax.axis_index("fsdp")
        c, x, y = rep % 2, (rep // 2) % 2, rep // 4
        w.rep, w.z, w.c, w.x, w.y = rep, z, c, x, y
        w.partner, w.xn, w.yn = {"rep": rep + 1 - 2 * c}, {"rep": rep + 2 - 4 * x}, {"rep": rep + 4 - 8 * y}
        w.zn = [{"fsdp": (z + d) % 4} for d in (1, 2, 3)]
        w.q, w.qx, w.qy, w.qd = y * 2 + x, y * 2 + 1 - x, (1 - y) * 2 + x, (1 - y) * 2 + 1 - x
        w.k, w.kx, w.ky, w.kd = c * 4 + w.q, c * 4 + w.qx, c * 4 + w.qy, c * 4 + w.qd
        o = (1 - c) * 4
        w.kp, w.kpx, w.kpy, w.kpd = o + w.q, o + w.qx, o + w.qy, o + w.qd

    def peers(w):
        return [w.partner, w.xn, w.yn] + w.zn


class Link:
    def __init__(g, w, sems):
        g.w, g.sems, g.ran, g.waiting = w, sems, [], False

    def copy(g, src, dst, s, r, dev):
        return pltpu.make_async_remote_copy(
            src_ref=src, dst_ref=dst, send_sem=s, recv_sem=r, device_id=dev, device_id_type=MESH
        )

    def send(g, u, i, src, dst, r, dev):
        cp = g.copy(src, dst, g.sems[0].at[u, i], r, dev)
        if g.waiting:
            cp.wait_send()
        else:
            cp.start()

    def got(g, ref, r):
        if not g.waiting:
            g.copy(ref, ref, g.sems[0].at[0, 0], r, g.w.partner).wait_recv()

    def add(g, ref, at, *parts):
        if not g.waiting:
            t = ref[at].astype(f32)
            for p, where in parts:
                t = t + p[where].astype(f32)
            ref[at] = t.astype(bf16)

    def step(g, name, u):
        getattr(g, name)(u)
        g.ran.append((name, u))

    def finish(g):
        g.waiting = True
        for name, u in g.ran:
            getattr(g, name)(u)


class Gather(Link):
    def __init__(g, w, own, W, sems):
        super().__init__(w, sems)
        g.own, g.W = own, W
        g.rz, g.rx, g.ry, g.rp = sems[1:]

    def reg(g, k, u, a=0, b=None):
        r0, n, h = GATHER_UNITS[u]
        return g.W.at[k, :, pl.ds(r0 + a, (n if b is None else b) - a)]

    def g0(g, u):
        r0, n, h = GATHER_UNITS[u]
        for d in range(3):
            src = g.own.at[g.w.k, pl.ds(r0, n)]
            g.send(u, d, src, g.W.at[g.w.k, d, pl.ds(r0, n)], g.rz.at[u, d], g.w.zn[d])

    def g1(g, u):
        r0, n, h = GATHER_UNITS[u]
        for d in range(3):
            g.got(g.W.at[g.w.k, d, pl.ds(r0, n)], g.rz.at[u, d])
        b = g.reg(g.w.k, u)
        g.send(u, 3, b, b, g.rx.at[u, 0], g.w.xn)
        g.send(u, 4, b, b, g.ry.at[u, 0], g.w.yn)
        g.send(u, 5, b, b, g.rp.at[u, 0], g.w.partner)

    def g2a(g, u):
        h = GATHER_UNITS[u][2]
        g.got(g.reg(g.w.kx, u), g.rx.at[u, 0])
        b = g.reg(g.w.kx, u, 0, h)
        g.send(u, 6, b, b, g.ry.at[u, 1], g.w.yn)
        b = g.reg(g.w.kx, u)
        g.send(u, 7, b, b, g.rp.at[u, 1], g.w.partner)

    def g2b(g, u):
        h = GATHER_UNITS[u][2]
        g.got(g.reg(g.w.ky, u), g.ry.at[u, 0])
        b = g.reg(g.w.ky, u, h)
        g.send(u, 8, b, b, g.rx.at[u, 1], g.w.xn)
        b = g.reg(g.w.ky, u)
        g.send(u, 9, b, b, g.rp.at[u, 2], g.w.partner)

    def g3(g, u):
        h = GATHER_UNITS[u][2]
        g.got(g.reg(g.w.kd, u, 0, h), g.ry.at[u, 1])
        g.got(g.reg(g.w.kd, u, h), g.rx.at[u, 1])
        b = g.reg(g.w.kd, u)
        g.send(u, 10, b, b, g.rp.at[u, 3], g.w.partner)

    def g4(g, u):
        for i, k in enumerate((g.w.kp, g.w.kpx, g.w.kpy, g.w.kpd)):
            g.got(g.reg(k, u), g.rp.at[u, i])


class Reduce(Link):
    def __init__(g, w, S, RX3, RY3, RX, RY, RZ, FIN, sems):
        super().__init__(w, sems)
        g.S, g.RX3, g.RY3, g.RX, g.RY, g.RZ, g.FIN = S, RX3, RY3, RX, RY, RZ, FIN
        g.r3, g.rxy, g.rz, g.rf, g.lf = sems[1:]

    def at(g, u):
        r0, n, h = REDUCE_UNITS[u]
        return pl.ds(r0, n), g.S(u), g.w

    def c1(g, u):
        R, S, w = g.at(u)
        g.send(u, 0, S.at[w.qd, 0:2], g.RX3.at[:, R], g.r3.at[u, 0], w.xn)
        g.send(u, 1, S.at[w.qd, 2:4], g.RY3.at[:, R], g.r3.at[u, 1], w.yn)
        g.send(u, 2, S.at[w.qx, 0:2], g.RX.at[0:2, R], g.rxy.at[u, 0], w.xn)
        g.send(u, 3, S.at[w.qy, 2:4], g.RY.at[2:4, R], g.rxy.at[u, 1], w.yn)

    def c2a(g, u):
        R, S, w = g.at(u)
        g.got(g.RY3.at[:, R], g.r3.at[u, 1])
        g.add(S, (w.qx, slice(2, 4)), (g.RY3, (slice(None), R)))
        g.send(u, 4, S.at[w.qx, 2:4], g.RX.at[2:4, R], g.rxy.at[u, 2], w.xn)

    def c2b(g, u):
        R, S, w = g.at(u)
        g.got(g.RX3.at[:, R], g.r3.at[u, 0])
        g.add(S, (w.qy, slice(0, 2)), (g.RX3, (slice(None), R)))
        g.send(u, 5, S.at[w.qy, 0:2], g.RY.at[0:2, R], g.rxy.at[u, 3], w.yn)

    def c3(g, u):
        R, S, w = g.at(u)
        g.got(g.RX.at[0:2, R], g.rxy.at[u, 0])
        g.got(g.RX.at[2:4, R], g.rxy.at[u, 2])
        g.got(g.RY.at[2:4, R], g.rxy.at[u, 1])
        g.got(g.RY.at[0:2, R], g.rxy.at[u, 3])
        g.add(S, (w.q,), (g.RX, (slice(None), R)), (g.RY, (slice(None), R)))
        for d in range(3):
            zt = (w.z + d + 1) % 4
            g.send(u, 6 + d, S.at[w.q, zt], g.RZ.at[d, R], g.rz.at[u, d], w.zn[d])

    def c4(g, u):
        R, S, w = g.at(u)
        for d in range(3):
            g.got(g.RZ.at[d, R], g.rz.at[u, d])
        g.add(S, (w.q, w.z), *[(g.RZ, (d, R)) for d in range(3)])
        src, dst = S.at[w.q, w.z], g.FIN.at[w.k, R]
        g.send(u, 9, src, dst, g.rf.at[u, 0], w.xn)
        g.send(u, 10, src, dst, g.rf.at[u, 1], w.yn)
        g.send(u, 11, src, dst, g.rf.at[u, 4], w.partner)
        if not g.waiting:
            pltpu.make_async_copy(src, dst, g.lf.at[u]).start()

    def fin(g, k, u, a=0, b=None):
        r0, n, h = REDUCE_UNITS[u]
        return g.FIN.at[k, pl.ds(r0 + a, (n if b is None else b) - a)]

    def c5a(g, u):
        h, w = REDUCE_UNITS[u][2], g.w
        g.got(g.fin(w.kx, u), g.rf.at[u, 0])
        b = g.fin(w.kx, u, 0, h)
        g.send(u, 12, b, b, g.rf.at[u, 3], w.yn)
        b = g.fin(w.kx, u)
        g.send(u, 13, b, b, g.rf.at[u, 5], w.partner)

    def c5b(g, u):
        h, w = REDUCE_UNITS[u][2], g.w
        g.got(g.fin(w.ky, u), g.rf.at[u, 1])
        b = g.fin(w.ky, u, h)
        g.send(u, 14, b, b, g.rf.at[u, 2], w.xn)
        b = g.fin(w.ky, u)
        g.send(u, 15, b, b, g.rf.at[u, 6], w.partner)

    def c6(g, u):
        h, w = REDUCE_UNITS[u][2], g.w
        g.got(g.fin(w.kd, u, 0, h), g.rf.at[u, 3])
        g.got(g.fin(w.kd, u, h), g.rf.at[u, 2])
        b = g.fin(w.kd, u)
        g.send(u, 16, b, b, g.rf.at[u, 7], w.partner)

    def c7(g, u):
        R, S, w = g.at(u)
        for i, k in enumerate((w.kp, w.kpx, w.kpy, w.kpd)):
            g.got(g.fin(k, u), g.rf.at[u, 4 + i])
        if not g.waiting:
            pltpu.make_async_copy(S.at[w.q, w.z], g.fin(w.k, u), g.lf.at[u]).wait()


def load_unit(w, own, W, dst, sem, u0, n, row0=0, halves=False):
    def block(k, _):
        def one(r, view, c0):
            def put(src, zs):
                rows = pl.ds(pl.multiple_of(row0 + zs * n, 16), n)
                pltpu.make_async_copy(src, view.at[rows, pl.ds(pl.multiple_of(c0, 128), 128)], sem).start()

            put(own.at[k, pl.ds(r, n)], w.z)
            for d in range(3):
                put(W.at[k, d, pl.ds(r, n)], (w.z + 3 - d) % 4)

        if halves:
            for s in range(2):
                one(u0 + s * n, dst.at[k // 4], (k % 4) * 256 + s * 128)
        else:
            one(u0, dst, k * 128)
        return 0

    lax.fori_loop(0, 8, block, 0)


def rope(t, c, s):
    first = (lanes() % 64) < 32
    return t * c + jnp.where(first, pltpu.roll(t, 96, 1), pltpu.roll(t, 32, 1)) * s


def dup(t, half):
    return jnp.where((lanes() < 64) == (half == 0), t, pltpu.roll(t, 64, 1))


def gain_row(tile):
    at = (lax.broadcasted_iota(jnp.int32, (8, 128), 0) == 0) & (lax.broadcasted_iota(jnp.int32, (8, 128), 1) == 0)
    return mm(at.astype(f32).astype(bf16), tile, NT)[0:1]


def norm(v, g):
    return v * lax.rsqrt(jnp.mean(v * v, axis=1, keepdims=True) + NORM_EPS) * g


def norm_back(v, g, u):
    r = lax.rsqrt(jnp.mean(v * v, axis=1, keepdims=True) + NORM_EPS)
    wv = u * g
    return r * wv - v * (r * r * r) * jnp.mean(wv * v, axis=1, keepdims=True), u * v * r


def head_at(h):
    t, half = h // 2, h % 2
    mine = (lanes() // 64) == half
    return t, h // 3, mine, pl.ds(pl.multiple_of(t * 128, 128), 128)


def head_fwd(h, qk, k2, v2, bias, ctx, lse):
    t, g, mine, col = head_at(h)
    hm = jnp.where(mine, 0.125, 0.0).astype(bf16)
    for i in range(2):
        rows, n = pl.ds(256 * i, 256), 256 * (i + 1)
        s = mm(qk[rows, col] * hm, k2[g, pl.ds(0, n)], NT) + bias[rows, pl.ds(0, n)].astype(f32)
        m = jnp.max(s, axis=1, keepdims=True)
        p = jnp.exp(s - m)
        l = jnp.sum(p, axis=1, keepdims=True)
        o = mm((p * (1.0 / l)).astype(bf16), v2[g, pl.ds(0, n)])
        ctx[rows, col] = jnp.where(mine, o, ctx[rows, col].astype(f32)).astype(bf16)
        lse[rows] = jnp.where(lanes() == h, m + jnp.log(l), lse[rows])


def head_bwd(h, qk, k2, v2, bias, lse, dctx, dq, dk, dv):
    t, g, mine, col = head_at(h)
    hm = jnp.where(mine, 0.125, 0.0).astype(bf16)
    om = jnp.where(mine, 1.0, 0.0).astype(bf16)
    for i in range(2):
        rows, n = pl.ds(256 * i, 256), 256 * (i + 1)
        qs = qk[rows, col] * hm
        do = dctx[t // 4, rows, pl.ds(pl.multiple_of((t % 4) * 128, 128), 128)] * om
        le = jnp.sum(jnp.where(lanes() == h, lse[rows], 0.0), axis=1, keepdims=True)
        s = mm(qs, k2[g, pl.ds(0, n)], NT) + bias[rows, pl.ds(0, n)].astype(f32)
        p = jnp.exp(s - le)
        dp = mm(do, v2[g, pl.ds(0, n)], NT)
        dv[g, pl.ds(0, n)] += mm(p.astype(bf16), do, TN)
        ds = (p * (dp - jnp.sum(p * dp, axis=1, keepdims=True))).astype(bf16)
        dk[g, pl.ds(0, n)] += mm(ds, qs, TN)
        dq[rows, col] = jnp.where(mine, mm(ds, k2[g, pl.ds(0, n)]) * 0.125, dq[rows, col])


KEYS = [(7, 1), (8, 0), (8, 1), (9, 0), (9, 1)]
VALUES = [(10, 0), (10, 1), (11, 0), (11, 1), (12, 0)]


def layer_kernel(
    tokT, cotT, freq, ids, own,
    boT, tgT, FIN, W, n1H, ctxH,
    cot, cos, sin, qk, k2, v2, lse, mid, n2, gains,
    wg, wd, bias, n2T, n2pT, cpT, dypp, hid, dgu, hidp, dgup, da, acc, dacc, dk, dv, gcol, gcolp,
    SM, SO, RX3, RY3, RX, RY, RZ,
    lsem, ps, pr, *sems,
):
    w = Where()
    c = w.c
    bar = pltpu.get_barrier_semaphore()
    for p in w.peers():
        pl.semaphore_signal(bar, inc=1, device_id=p, device_id_type=MESH)
    tl = pltpu.make_async_copy(tokT, tgT, lsem.at[0])
    tl.start()
    cl = pltpu.make_async_copy(cotT, boT, lsem.at[1])
    cl.start()
    pl.semaphore_wait(bar, 6)
    ga = Gather(w, own, W, sems[:5])
    re = Reduce(w, lambda u: SM.at[u] if u < 5 else SO.at[u - 5], RX3, RY3, RX, RY, RZ, FIN, sems[5:])
    live, local = {}, {}

    def psend(i, src, dst):
        live[i] = ga.copy(src, dst, ps.at[i], pr.at[i], w.partner)
        live[i].start()

    def psent(*which):
        for i in which:
            live.pop(i).wait_send()

    def pgot(i, dst):
        ga.copy(dst, dst, ps.at[0], pr.at[i], w.partner).wait_recv()

    def begin(name, src, dst, sem):
        local[name] = pltpu.make_async_copy(src, dst, sem)
        local[name].start()

    def end(name):
        local.pop(name).wait()

    other = pl.ds(pl.multiple_of((1 - c) * 512, 512), 512)
    mine = pl.ds(pl.multiple_of(c * 512, 512), 512)
    half_rows = [pl.ds(256 * i, 256) for i in range(2)]

    def A0():
        seq = ids[...].astype(f32)
        column = jnp.swapaxes(jnp.broadcast_to(seq, (8, 512)), 0, 1)[:, 0:1]
        for i in range(2):
            own_seq = column[256 * i : 256 * (i + 1)]
            rows = lax.broadcasted_iota(jnp.int32, (256, 512), 0) + 256 * i
            cols = lax.broadcasted_iota(jnp.int32, (256, 512), 1)
            ok = (own_seq == seq) & (cols <= rows)
            bias[pl.ds(256 * i, 256)] = jnp.where(ok, 0.0, NEG_LARGE).astype(bf16)
            first_row = jnp.sum(jnp.where(seq < own_seq, 1.0, 0.0), axis=1, keepdims=True)
            row = (lax.broadcasted_iota(jnp.int32, (256, 1), 0) + 256 * i).astype(f32)
            angle = (row - first_row) * freq[...]
            cos[pl.ds(256 * i, 256)] = jnp.cos(angle)
            sin[pl.ds(256 * i, 256)] = jnp.where((lanes() % 64) < 32, -1.0, 1.0) * jnp.sin(angle)
        lse[...] = jnp.zeros_like(lse)
        acc[...] = jnp.zeros_like(acc)
        dacc[...] = jnp.zeros_like(dacc)
        dk[...] = jnp.zeros_like(dk)
        dv[...] = jnp.zeros_like(dv)
        tl.wait()
        cl.wait()
        mid[...] = jnp.swapaxes(tgT[...], 0, 1).astype(f32)
        cot[:, 896:1024] = jnp.zeros((512, 128), bf16)
        cot[:, 0:960] = jnp.swapaxes(boT[...], 0, 1)

    def LQ():
        load_unit(w, own, W, wg, lsem.at[0], 0, 240, halves=True)

    def wait_q():
        pltpu.make_async_copy(wg, wg, lsem.at[0]).wait()

    def LO():
        load_unit(w, own, W, wd, lsem.at[1], 480, 240)

    def wait_o():
        view = wd.at[pl.ds(0, 960)]
        pltpu.make_async_copy(view, view, lsem.at[1]).wait()

    def A1():
        wait_q()
        gains[...] = jnp.zeros_like(gains)
        gains[0:1] = gain_row(wg[0, :, 896:1024])
        gains[1:2] = gain_row(wg[1, :, 896:1024])
        n1 = norm(mid[...], gains[0:1]).astype(bf16)
        da[:, 0:960] = n1
        tgT[...] = jnp.swapaxes(n1, 0, 1)
        for half, (lo, hi) in enumerate(((0, 6), (6, 13))):
            res = mm(da[:, 0:960], wg[half, :, 0 : (hi - lo) * 128])
            for t in range(lo, hi):
                tile = res[:, (t - lo) * 128 : (t - lo + 1) * 128]
                if t < 10:
                    tile = rope(tile, cos[...], sin[...])
                    qk[:, t * 128 : (t + 1) * 128] = tile.astype(bf16)
                for i in range(5):
                    if KEYS[i][0] == t:
                        k2[i] = dup(tile, KEYS[i][1]).astype(bf16)
                    if VALUES[i][0] == t:
                        v2[i] = dup(tile, VALUES[i][1]).astype(bf16)
        begin("n1", tgT, n1H, lsem.at[2])
        da[...] = jnp.zeros_like(da)

    def A3():
        wait_o()
        for rows in half_rows:
            m = mid[rows] + mm(da[rows, 0:960], wd[pl.ds(0, 960), 0:960])
            mid[rows] = m
            n2[rows] = norm(m, gains[1:2]).astype(bf16)
        n2T[...] = jnp.swapaxes(n2[...], 0, 1)
        boT[...] = jnp.swapaxes(da[:, 0:960], 0, 1)
        psend(0, n2T, n2pT)
        psend(1, cot.at[:, other], dypp)
        psend(2, boT, cpT)
        begin("ctx", boT, ctxH, lsem.at[3])

    def dslot(j):
        return pl.ds(pl.multiple_of(((j + 2) % 3) * 512, 512), 512)

    def L(j):
        load_unit(w, own, W, wg.at[j % 2], lsem.at[4 + j % 2], 720 + 368 * j, 240)
        load_unit(w, own, W, wd, lsem.at[6 + j % 2], 960 + 368 * j, 128, row0=((j + 2) % 3) * 512)

    def sends(j):
        b = j % 2
        return (
            ga.copy(hid.at[b], hidp.at[b], ps.at[4 + j], pr.at[4 + j], w.partner),
            ga.copy(dgu.at[b, 1 - c], dgup.at[b], ps.at[9 + j], pr.at[9 + j], w.partner),
        )

    def F(j):
        b = j % 2
        pltpu.make_async_copy(wg.at[b], wg.at[b], lsem.at[4 + b]).wait()
        view = wd.at[dslot(j)]
        pltpu.make_async_copy(view, view, lsem.at[6 + b]).wait()

        @pl.when(j >= 2)
        def _():
            sends(j - 2)[0].wait_send()
            sends(j - 2)[1].wait_send()

        def half(i, _):
            rows = pl.ds(pl.multiple_of(i * 256, 256), 256)
            gu = mm(n2[rows], wg[b])
            gate, up = gu[:, :512], gu[:, 512:]
            sg = jax.nn.sigmoid(gate)
            a = gate * sg
            hb = (a * up).astype(bf16)
            hid[b, rows] = hb
            acc[rows, 0:960] += mm(hb, wd[dslot(j), 0:960])
            dh = mm(cot[rows, 0:960], wd[dslot(j), 0:960], NT)
            dgate = (dh * up * (sg * (1.0 + gate * (1.0 - sg)))).astype(bf16)
            dup_ = (dh * a).astype(bf16)
            dgu[b, 0, rows] = dgate
            dgu[b, 1, rows] = dup_
            dacc[rows] += mm(dgate, wg[b, :, 0:512], NT) + mm(dup_, wg[b, :, 512:1024], NT)
            return 0

        lax.fori_loop(0, 2, half, 0)
        for cp in sends(j):
            cp.start()

    def cut(S, G, n, r0=0):
        for q in range(4):
            for z in range(4):
                S[q, z, r0 : r0 + n] = G[z * n : (z + 1) * n, q * 128 : (q + 1) * 128].astype(bf16)

    def R(j):
        b = j % 2

        @pl.when(j == 0)
        def _():
            pgot(0, n2pT)
            pgot(1, dypp)

        pgot(4 + j, hidp.at[b])
        pgot(9 + j, dgup.at[b])
        cut(SM.at[j], mm(n2T[...], dgu[b, c]) + mm(n2pT[...], dgup[b]), 240)
        cut(SM.at[j], mm(hid[b], cot[:, mine], TN) + mm(hidp[b], dypp[...], TN), 128, 240)

    def B1():
        for cp in sends(3) + sends(4):
            cp.wait_send()
        psent(0, 1, 2)
        LO()
        LQ()
        end("ctx")
        begin("ctxT", ctxH, n2T, lsem.at[3])
        ones = jnp.ones((256, 128), bf16)
        da[:, 896:1024] = jnp.zeros((512, 128), bf16)
        gc = 0.0
        for i, rows in enumerate(half_rows):
            m = mid[rows]
            boT[:, 256 * i : 256 * (i + 1)] = jnp.swapaxes((m + acc[rows, 0:960]).astype(bf16), 0, 1)
            dv_, gp = norm_back(m, gains[1:2], dacc[rows])
            dmid = cot[rows, 0:960].astype(f32) + dv_
            dacc[rows] = dmid
            da[rows, 0:960] = dmid.astype(bf16)
            gc = gc + mm(gp.astype(bf16), ones, TN)
        gcol[1] = gc.astype(bf16)
        psend(14, da.at[:, other], hidp.at[1])

    def B2():
        wait_o()
        hid[1, :, 384:512] = jnp.zeros((512, 128), bf16)
        hid[0] = mm(da[:, 0:960], wd[pl.ds(0, 512), 0:960], NT).astype(bf16)
        hid[1, :, 0:448] = mm(da[:, 0:960], wd[pl.ds(512, 448), 0:960], NT).astype(bf16)
        end("ctxT")
        pgot(2, cpT)
        pgot(14, hidp.at[1])
        end("n1")
        psend(3, n1H, n2pT)
        cut(SO.at[0], mm(n2T[...], da[:, mine]) + mm(cpT[...], hidp[1]), 240)
        acc[...] = jnp.zeros_like(acc)
        psent(14)
        begin("n1T", n1H, n2T, lsem.at[2])
        begin("tok", tokT, tgT, lsem.at[3])

    def D1():
        def put(half, t, tile):
            dgu[half, t // 4, :, (t % 4) * 128 : (t % 4 + 1) * 128] = tile.astype(bf16)

        first = lanes() < 64
        nsin = -sin[...]

        def fold(ref, i):
            return ref[i] + pltpu.roll(ref[i], 64, 1)

        for t in range(7):
            put(t // 6, t % 6, rope(acc[:, t * 128 : (t + 1) * 128], cos[...], nsin))
        zero = jnp.zeros((512, 128), f32)
        for half, t in ((0, 6), (0, 7), (1, 7)):
            put(half, t, zero)
        kk, vv = [fold(dk, i) for i in range(5)], [fold(dv, i) for i in range(5)]
        put(1, 1, rope(jnp.where(first, acc[:, 896:1024], kk[0]), cos[...], nsin))
        put(1, 2, rope(jnp.where(first, kk[1], kk[2]), cos[...], nsin))
        put(1, 3, rope(jnp.where(first, kk[3], kk[4]), cos[...], nsin))
        put(1, 4, jnp.where(first, vv[0], vv[1]))
        put(1, 5, jnp.where(first, vv[2], vv[3]))
        put(1, 6, jnp.where(first, vv[4], 0.0))
        psend(15, dgu.at[1 - c], dgup)

    def qgrad(sub):
        for q in range(4):
            t = 2 * q + sub
            if t == 7:
                G = gcol[c].astype(f32) + gcolp[...].astype(f32)
            else:
                at = slice((t % 4) * 128, (t % 4 + 1) * 128)
                G = mm(n2T[...], dgu[c, t // 4, :, at]) + mm(n2pT[...], dgup[t // 4, :, at])
            for z in range(4):
                SO[1 + sub, q, z] = G[z * 240 : (z + 1) * 240].astype(bf16)

    def D2():
        end("n1T")
        pgot(3, n2pT)
        pgot(15, dgup)
        qgrad(0)

    def D3():
        wait_q()
        end("tok")
        da[:, 0:960] = jnp.swapaxes(tgT[...], 0, 1)
        ones = jnp.ones((256, 128), bf16)
        gc = 0.0
        for i, rows in enumerate(half_rows):
            dn1 = mm(dgu[0, 0, rows], wg[0, :, 0:512], NT) + mm(dgu[0, 1, rows, 0:256], wg[0, :, 512:768], NT)
            dn1 += mm(dgu[1, 0, rows], wg[1, :, 0:512], NT) + mm(dgu[1, 1, rows, 0:384], wg[1, :, 512:896], NT)
            dv_, gp = norm_back(da[rows, 0:960].astype(f32), gains[0:1], dn1)
            tgT[:, 256 * i : 256 * (i + 1)] = jnp.swapaxes((dacc[rows] + dv_).astype(bf16), 0, 1)
            gc = gc + mm(gp.astype(bf16), ones, TN)
        gcol[0] = gc.astype(bf16)
        psend(16, gcol.at[1 - c], gcolp)

    def D4():
        pgot(16, gcolp)
        qgrad(1)

    steps = dict(A0=A0, LQ=LQ, A1=A1, LO=LO, A3=A3, L=L, B1=B1, B2=B2, D1=D1, D2=D2, D3=D3, D4=D4)

    def run(part):
        for name, at in part:
            if name in steps:
                steps[name](*([] if at is None else [at]))
            else:
                (ga if name[0] == "g" else re).step(name, at)

    def after(i, parts, at=None):
        for n, part in enumerate(parts):
            if part:
                pl.when(i == (n if at is None else at(n)))(lambda part=part: run(part))

    def heads(one_head, parts):
        def turn(h, _):
            one_head(h)
            after(h, parts, lambda n: 3 * n + 2)
            return 0

        lax.fori_loop(0, 15, turn, 0)

    def unit(j, _):
        F(j)
        after(j, PARTS["F"])
        R(j)
        after(j, PARTS["R"])
        return 0

    run(PARTS["start"])
    heads(lambda h: head_fwd(h, qk, k2, v2, bias, da, lse), PARTS["H"])
    run(PARTS["A3"])
    lax.fori_loop(0, 5, unit, 0)
    run(PARTS["B1"])
    heads(lambda h: head_bwd(h, qk, k2, v2, bias, lse, hid, acc, dk, dv), PARTS["K"])
    run(PARTS["D1"])
    for i in list(live):
        psent(i)
    ga.finish()
    re.finish()


def layer(tok, cot, ids, own):
    freq = ROPE_BASE ** (-2.0 * (jnp.arange(128) % 32).astype(f32) / HEAD)
    S, D = jax.ShapeDtypeStruct, pltpu.SemaphoreType.DMA

    def V(*shape, dt=bf16):
        return pltpu.VMEM(shape, dt)

    vm = pl.BlockSpec(memory_space=pltpu.VMEM)
    hb = pl.BlockSpec(memory_space=pl.ANY)
    outs = pl.pallas_call(
        layer_kernel,
        name="layer",
        out_shape=[
            S((960, 512), bf16), S((960, 512), bf16), S((8, ROWS, 128), bf16),
            S((8, 3, ROWS, 128), bf16), S((960, 512), bf16), S((960, 512), bf16),
        ],
        in_specs=[hb, hb, vm, vm, hb],
        out_specs=[vm, vm, hb, hb, hb, hb],
        scratch_shapes=[
            V(512, 1024), V(512, 128, dt=f32), V(512, 128, dt=f32), V(512, 1280), V(5, 512, 128), V(5, 512, 128), V(512, 128, dt=f32), V(512, 960, dt=f32),
            V(512, 960), V(8, 960, dt=f32),
            V(2, 960, 1024), V(1536, 1024), V(512, 512), V(960, 512), V(960, 512), V(960, 512), V(512, 512),
            V(2, 512, 512), V(2, 2, 512, 512), V(2, 512, 512), V(2, 512, 512), V(512, 1024),
            V(512, 1024, dt=f32), V(512, 960, dt=f32), V(5, 512, 128, dt=f32), V(5, 512, 128, dt=f32),
            V(2, 960, 128), V(960, 128),
            V(5, 4, 4, 368, 128), V(3, 4, 4, 240, 128),
            V(2, ROWS, 128), V(2, ROWS, 128), V(4, ROWS, 128), V(4, ROWS, 128), V(3, ROWS, 128),
            D((8,)), D((17,)), D((17,)),
            D((8, 11)), D((8, 3)), D((8, 2)), D((8, 2)), D((8, 4)),
            D((8, 17)), D((8, 2)), D((8, 4)), D((8, 3)), D((8, 8)), D((8,)),
        ],
        compiler_params=pltpu.CompilerParams(
            collective_id=0, has_side_effects=True, vmem_limit_bytes=67043328
        ),
    )(tok.T, cot.T, freq[None, :], ids[None, :], own)
    return outs[:3]


PARTS = {
    "start": [
        ("g0", 0), ("g0", 1), ("g0", 2), ("g0", 3), ("A0", None), ("g1", 0), ("g0", 4), ("g1", 1), ("g0", 5),
        ("g2a", 0), ("g2b", 0), ("g1", 2), ("g0", 6), ("g2a", 1), ("g2b", 1), ("g3", 0), ("g4", 0),
        ("g2a", 2), ("g2b", 2), ("g1", 3), ("g0", 7), ("g3", 1), ("g4", 1), ("LQ", None), ("g3", 2),
        ("g4", 2), ("LO", None), ("g1", 4), ("A1", None), ("g2a", 3), ("g2b", 3),
    ],
    "H": [
        [
            ("g2a", 4), ("g2b", 4), ("g1", 5),
        ],
        [
            ("g3", 3),
        ],
        [
            ("g3", 4), ("g1", 6), ("g4", 3), ("L", 0),
        ],
        [
            ("g4", 4),
        ],
        [
            ("g2a", 5), ("g2b", 5),
        ],
    ],
    "A3": [
        ("A3", None), ("L", 1), ("g1", 7),
    ],
    "F": [
        [
            ("g3", 5), ("g2a", 6), ("g2b", 6),
        ],
        [
            ("g3", 6), ("g2a", 7), ("g2b", 7),
        ],
        [],
        [
            ("c3", 0), ("c2a", 1), ("c2b", 1), ("g4", 7), ("L", 4),
        ],
        [
            ("c2a", 2), ("c2b", 2),
        ],
    ],
    "R": [
        [
            ("c1", 0), ("g4", 5), ("L", 2),
        ],
        [
            ("c2a", 0), ("c2b", 0), ("c1", 1), ("g4", 6), ("L", 3),
        ],
        [
            ("g3", 7), ("c1", 2),
        ],
        [
            ("c1", 3),
        ],
        [
            ("c4", 0), ("c1", 4),
        ],
    ],
    "B1": [
        ("B1", None), ("c3", 1), ("B2", None), ("c2a", 3), ("c2b", 3), ("c1", 5),
    ],
    "K": [
        [],
        [
            ("c4", 1), ("c5a", 0), ("c3", 2),
        ],
        [
            ("c5b", 0), ("c2b", 4), ("c2a", 4),
        ],
        [],
        [
            ("c4", 2), ("c3", 3),
        ],
    ],
    "D1": [
        ("D1", None), ("c2a", 5), ("c2b", 5), ("D2", None), ("c5a", 1), ("c1", 6), ("D3", None), ("c6", 0),
        ("c5b", 1), ("D4", None), ("c1", 7), ("c4", 3), ("c3", 4), ("c5a", 2), ("c7", 0), ("c5b", 2),
        ("c3", 5), ("c2b", 6), ("c2a", 6), ("c6", 1), ("c7", 1), ("c4", 4), ("c2b", 7), ("c2a", 7),
        ("c5a", 3), ("c4", 5), ("c5b", 3), ("c6", 2), ("c7", 2), ("c3", 6), ("c5a", 4), ("c5b", 4), ("c3", 7),
        ("c5a", 5), ("c6", 3), ("c7", 3), ("c5b", 5), ("c6", 4), ("c4", 6), ("c7", 4), ("c6", 5), ("c7", 5),
        ("c5a", 6), ("c5b", 6), ("c4", 7), ("c6", 6), ("c7", 6), ("c5a", 7), ("c5b", 7), ("c6", 7), ("c7", 7),
    ],
}


def on_device(tokens, sequence_ids, cotangent, norm_gains, qkv_weight, out_weight, gate_up_weight, down_weight, *moments):
    weights = (norm_gains, qkv_weight, out_weight, gate_up_weight, down_weight)
    block_out, tokens_grad, packed = layer(tokens, cotangent, sequence_ids, pack(*weights))
    return (block_out.T, tokens_grad.T, *adam(packed, weights, moments))


def solution(mesh):
    fits = mesh.shape["rep"] == 8 and mesh.shape["fsdp"] == 4
    return jax.shard_map(
        on_device if fits else on_device_any,
        mesh=mesh,
        in_specs=(
            P(("rep", "fsdp"), None),
            P(("rep", "fsdp")),
            P(("rep", "fsdp"), None),
            P(None, "fsdp"),
            P("fsdp", None),
            P("fsdp", None),
            P("fsdp", None),
            P("fsdp", None),
            P(None, "fsdp"),
            P("fsdp", None),
            P("fsdp", None),
            P("fsdp", None),
            P("fsdp", None),
            P(None, "fsdp"),
            P("fsdp", None),
            P("fsdp", None),
            P("fsdp", None),
            P("fsdp", None),
        ),
        out_specs=(
            P(("rep", "fsdp"), None),
            P(("rep", "fsdp"), None),
            P(None, "fsdp"),
            P("fsdp", None),
            P("fsdp", None),
            P("fsdp", None),
            P("fsdp", None),
            P(None, "fsdp"),
            P("fsdp", None),
            P("fsdp", None),
            P("fsdp", None),
            P("fsdp", None),
            P(None, "fsdp"),
            P("fsdp", None),
            P("fsdp", None),
            P("fsdp", None),
            P("fsdp", None),
            P(None, "fsdp"),
            P("fsdp", None),
            P("fsdp", None),
            P("fsdp", None),
            P("fsdp", None),
        ),
        check_vma=False,
    )
```

profile of v0, /device:TPU:0, one launch (start us, length us, event | category | flops | bytes accessed | tf_op | source)
XLA Modules:
  0.0 252.5 jit_solution(4746827536488956074)
XLA Ops:
  0.7 0.5 fusion.2.freq
  1.2 8.7 %pack.1.own = bf16[8,2560,128]{2,1,0:T(8,128)(2,1)} custom-call(f32[2,240]{1,0:T(2,128)} %refs_0_.1, f32[240,1600]{1,0:T(8,128)} %refs_1_.1, f32[240,960]{1,0:T(8,128)} %refs_2_.1, f32[240,5120]{1,0:T(8,128)} %refs_3_.1, f32[960,640]{1,0:T(8,128)} %bitcast.12), custom_call_target="tpu_custom_call" | custom-call | tf_op jit(solution)/shard_map/pack/pallas_call | solution.py:411
  9.9 210.7 %layer.1 = (bf16[960,512]{1,0:T(8,128)(2,1)}, bf16[960,512]{1,0:T(8,128)(2,1)}, bf16[8,2560,128]{2,1,0:T(8,128)(2,1)}, bf16[8,3,2560,128]{3,2,1,0:T(8,128)(2,1)}...) custom-call(bf16[960,512]{1,0:T(8,128)(2,1)} %bitcast.16, bf16[960,512]{1,0:T(8,128)(2,1)} %bitcast.17, ...), custom_call_target="tpu_custom_call" | custom-call | tf_op jit(solution)/shard_map/layer/pallas_call | solution.py:1087
  220.6 0.0 copy-start.1
  220.6 29.4 %adam.1 = (f32[2,240]{1,0:T(2,128)}, f32[240,1600]{1,0:T(8,128)}, f32[240,960]{1,0:T(8,128)}, f32[240,5120]{1,0:T(8,128)}, f32[960,640]{1,0:T(8,128)}, /*index=5...) custom-call(bf16[8,2560,128]{2,1,0:T(8,128)(2,1)} %get-tuple-element, ...), custom_call_target="tpu_custom_call" | custom-call | tf_op jit(solution)/shard_map/adam/pallas_call | solution.py:465
  250.0 0.0 copy-start
  250.0 0.0 copy-done.1
  250.1 0.9 copy.42
  251.0 0.6 copy-done
  251.6 0.9 copy.43
Async XLA Ops:
  220.6 29.5 %copy-start.1 = (bf16[960,512]{1,0:T(8,128)(2,1)S(1)}, bf16[960,512]{1,0:T(8,128)(2,1)}, u32[]{:S(2)}) copy-start(bf16[960,512]{1,0:T(8,128)(2,1)} %get-tuple-element.45) | copy-start | bytes 2949124
  250.0 1.6 copy-start
where the time goes:
time: 255 us; the launch traced here: 253 us
  Pallas kernels  249 us (98%)
    pallas_call x1, Pallas kernels, layer(): pl.pallas_call(layer_kernel, name='layer', out_shape=[S((960, 512), bf16)...  211 us
    pallas_call x1, Pallas kernels, adam(): pl.pallas_call(adam_kernel, name='adam', grid=(8,), out_shape=shapes, in_...  29.4 us
    pallas_call x1, Pallas kernels, pack(): pl.pallas_call(pack_kernel, name='pack', grid=(8,), out_shape=jax.ShapeDt...  8.71 us

commit v1 on v0

--- a/solution.py
+++ b/solution.py
@@ -360,8 +360,8 @@
 MESH = pl.DeviceIdType.MESH
 bf16, f32 = jnp.bfloat16, jnp.float32
 ROWS = 2560
-GATHER_UNITS = [(0, 240, 128), (240, 240, 128), (480, 240, 128)] + [(720 + 368 * j, 368, 192) for j in range(5)]
-REDUCE_UNITS = [(720 + 368 * j, 368, 192) for j in range(5)] + [(480, 240, 128), (0, 240, 128), (240, 240, 128)]
+GATHER_UNITS = [(0, 128, 64), (128, 112, 64), (240, 240, 128), (480, 240, 128)] + [(720 + 368 * j, 368, 192) for j in range(5)]
+REDUCE_UNITS = [(720 + 368 * j, 368, 192) for j in range(5)] + [(480, 240, 128), (0, 240, 128), (240, 128, 64), (368, 112, 64)]
 NT = (((1,), (1,)), ((), ()))
 NN = (((1,), (0,)), ((), ()))
 TN = (((0,), (0,)), ((), ()))
@@ -403,8 +403,8 @@
     own[0, 480:720] = jnp.where(lanes() < 960 - k * 128, out[...], 0.0).astype(bf16)
     for j in range(5):
         own[0, 720 + 368 * j : 960 + 368 * j] = gu[:, j * 128 : (j + 1) * 128].astype(bf16)
-        t = jnp.swapaxes(dnT[:, j * 128 : (j + 1) * 128], 0, 1)
-        own[0, 960 + 368 * j : 1088 + 368 * j] = jnp.where(lanes() < 960 - k * 128, t, 0.0).astype(bf16)
+        t = jnp.swapaxes(dnT[:, j * 128 : (j + 1) * 128].astype(bf16), 0, 1)
+        own[0, 960 + 368 * j : 1088 + 368 * j] = jnp.where(lanes() < 960 - k * 128, t.astype(f32), 0.0).astype(bf16)
 
 
 def pack(norm_gains, qkv, out, gu, down):
@@ -427,7 +427,9 @@
     def update(i, at, g, rate):
         m = BETA_ONE * first[i][at] + (1.0 - BETA_ONE) * g
         v = BETA_TWO * second[i][at] + (1.0 - BETA_TWO) * g * g
-        step = m * (1.0 / (1.0 - BETA_ONE**STEP)) / (jnp.sqrt(v * (1.0 / (1.0 - BETA_TWO**STEP))) + ADAM_EPS)
+        fixed = v * (1.0 / (1.0 - BETA_TWO**STEP))
+        root = fixed * lax.rsqrt(fixed)
+        step = m * (1.0 / (1.0 - BETA_ONE**STEP)) / (root + ADAM_EPS)
         if rate:
             step = step + rate * weight[i][at]
         grad[i][at] = g
@@ -453,7 +455,8 @@
     for j in range(5):
         c = slice(j * 128, (j + 1) * 128)
         update(3, (every, c), rows(720 + 368 * j, 960 + 368 * j), DECAY_RATE)
-        update(4, (every, c), jnp.swapaxes(rows(960 + 368 * j, 1088 + 368 * j), 0, 1), DECAY_RATE)
+        turned = jnp.swapaxes(FIN[0, 960 + 368 * j : 1088 + 368 * j], 0, 1).astype(f32)
+        update(4, (every, c), turned, DECAY_RATE)
 
 
 def adam(FIN, weights, moments):
@@ -479,6 +482,7 @@
         c, x, y = rep % 2, (rep // 2) % 2, rep // 4
         w.rep, w.z, w.c, w.x, w.y = rep, z, c, x, y
         w.partner, w.xn, w.yn = {"rep": rep + 1 - 2 * c}, {"rep": rep + 2 - 4 * x}, {"rep": rep + 4 - 8 * y}
+        w.dn = {"rep": rep + 6 - 4 * x - 8 * y}
         w.zn = [{"fsdp": (z + d) % 4} for d in (1, 2, 3)]
         w.q, w.qx, w.qy, w.qd = y * 2 + x, y * 2 + 1 - x, (1 - y) * 2 + x, (1 - y) * 2 + 1 - x
         w.k, w.kx, w.ky, w.kd = c * 4 + w.q, c * 4 + w.qx, c * 4 + w.qy, c * 4 + w.qd
@@ -486,7 +490,7 @@
         w.kp, w.kpx, w.kpy, w.kpd = o + w.q, o + w.qx, o + w.qy, o + w.qd
 
     def peers(w):
-        return [w.partner, w.xn, w.yn] + w.zn
+        return [w.partner, w.xn, w.yn, w.dn] + w.zn
 
 
 class Link:
@@ -588,6 +592,54 @@
     def at(g, u):
         r0, n, h = REDUCE_UNITS[u]
         return pl.ds(r0, n), g.S(u), g.w
+
+    def z1(g, u):
+        R, S, w = g.at(u)
+        landing = ((slice(0, 4), g.RX), (slice(0, 4), g.RY), (slice(0, 2), g.RX3), (slice(2, 4), g.RY3))
+        for i, (part, buf) in enumerate(landing):
+            d = min(i, 2)
+            g.send(u, i, S.at[part, (w.z + d + 1) % 4], buf.at[:, R], g.rxy.at[u, i], w.zn[d])
+
+    def z2(g, u):
+        r0, n, h = REDUCE_UNITS[u]
+        R, S, w = g.at(u)
+        for i, buf in enumerate((g.RX, g.RY, g.RX3, g.RY3)):
+            g.got(buf.at[:, R], g.rxy.at[u, i])
+        for a, third in ((0, g.RX3), (2, g.RY3)):
+            part = slice(a, a + 2)
+            g.add(S, (part, w.z), (g.RX, (part, R)), (g.RY, (part, R)), (third, (slice(None), R)))
+        up, low = (pl.ds(0, h), pl.ds(r0, h)), (pl.ds(h, n - h), pl.ds(r0 + h, n - h))
+        g.send(u, 4, S.at[w.qd, w.z, up[0]], g.RZ.at[0, up[1]], g.r3.at[u, 0], w.xn)
+        g.send(u, 5, S.at[w.qd, w.z, low[0]], g.RZ.at[0, low[1]], g.r3.at[u, 1], w.yn)
+        g.send(u, 6, S.at[w.qx, w.z, up[0]], g.RZ.at[1, up[1]], g.rz.at[u, 0], w.xn)
+        g.send(u, 7, S.at[w.qy, w.z, low[0]], g.RZ.at[2, low[1]], g.rz.at[u, 1], w.yn)
+
+    def z3a(g, u):
+        r0, n, h = REDUCE_UNITS[u]
+        R, S, w = g.at(u)
+        low = (pl.ds(h, n - h), pl.ds(r0 + h, n - h))
+        g.got(g.RZ.at[0, low[1]], g.r3.at[u, 1])
+        g.add(S, (w.qx, w.z, low[0]), (g.RZ, (0, low[1])))
+        g.send(u, 8, S.at[w.qx, w.z, low[0]], g.RZ.at[1, low[1]], g.rz.at[u, 2], w.xn)
+
+    def z3b(g, u):
+        r0, n, h = REDUCE_UNITS[u]
+        R, S, w = g.at(u)
+        up = (pl.ds(0, h), pl.ds(r0, h))
+        g.got(g.RZ.at[0, up[1]], g.r3.at[u, 0])
+        g.add(S, (w.qy, w.z, up[0]), (g.RZ, (0, up[1])))
+        g.send(u, 17, S.at[w.qy, w.z, up[0]], g.RZ.at[2, up[1]], g.rz.at[u, 3], w.yn)
+
+    def z4(g, u):
+        r0, n, h = REDUCE_UNITS[u]
+        R, S, w = g.at(u)
+        up, low = pl.ds(r0, h), pl.ds(r0 + h, n - h)
+        g.got(g.RZ.at[1, up], g.rz.at[u, 0])
+        g.got(g.RZ.at[1, low], g.rz.at[u, 2])
+        g.got(g.RZ.at[2, low], g.rz.at[u, 1])
+        g.got(g.RZ.at[2, up], g.rz.at[u, 3])
+        g.add(S, (w.q, w.z), (g.RZ, (1, R)), (g.RZ, (2, R)))
+        g.share(u)
 
     def c1(g, u):
         R, S, w = g.at(u)
@@ -624,7 +676,13 @@
         for d in range(3):
             g.got(g.RZ.at[d, R], g.rz.at[u, d])
         g.add(S, (w.q, w.z), *[(g.RZ, (d, R)) for d in range(3)])
+        g.share(u)
+
+    def share(g, u):
+        R, S, w = g.at(u)
         src, dst = S.at[w.q, w.z], g.FIN.at[w.k, R]
+        if u in DIAGONAL:
+            g.send(u, 12, src, dst, g.rf.at[u, 2], w.dn)
         g.send(u, 9, src, dst, g.rf.at[u, 0], w.xn)
         g.send(u, 10, src, dst, g.rf.at[u, 1], w.yn)
         g.send(u, 11, src, dst, g.rf.at[u, 4], w.partner)
@@ -638,23 +696,28 @@
     def c5a(g, u):
         h, w = REDUCE_UNITS[u][2], g.w
         g.got(g.fin(w.kx, u), g.rf.at[u, 0])
-        b = g.fin(w.kx, u, 0, h)
-        g.send(u, 12, b, b, g.rf.at[u, 3], w.yn)
+        if u not in DIAGONAL:
+            b = g.fin(w.kx, u, 0, h)
+            g.send(u, 12, b, b, g.rf.at[u, 3], w.yn)
         b = g.fin(w.kx, u)
         g.send(u, 13, b, b, g.rf.at[u, 5], w.partner)
 
     def c5b(g, u):
         h, w = REDUCE_UNITS[u][2], g.w
         g.got(g.fin(w.ky, u), g.rf.at[u, 1])
-        b = g.fin(w.ky, u, h)
-        g.send(u, 14, b, b, g.rf.at[u, 2], w.xn)
+        if u not in DIAGONAL:
+            b = g.fin(w.ky, u, h)
+            g.send(u, 14, b, b, g.rf.at[u, 2], w.xn)
         b = g.fin(w.ky, u)
         g.send(u, 15, b, b, g.rf.at[u, 6], w.partner)
 
     def c6(g, u):
         h, w = REDUCE_UNITS[u][2], g.w
-        g.got(g.fin(w.kd, u, 0, h), g.rf.at[u, 3])
-        g.got(g.fin(w.kd, u, h), g.rf.at[u, 2])
+        if u in DIAGONAL:
+            g.got(g.fin(w.kd, u), g.rf.at[u, 2])
+        else:
+            g.got(g.fin(w.kd, u, 0, h), g.rf.at[u, 3])
+            g.got(g.fin(w.kd, u, h), g.rf.at[u, 2])
         b = g.fin(w.kd, u)
         g.send(u, 16, b, b, g.rf.at[u, 7], w.partner)
 
@@ -714,39 +777,49 @@
 def head_at(h):
     t, half = h // 2, h % 2
     mine = (lanes() // 64) == half
-    return t, h // 3, mine, pl.ds(pl.multiple_of(t * 128, 128), 128)
-
-
-def head_fwd(h, qk, k2, v2, bias, ctx, lse):
-    t, g, mine, col = head_at(h)
-    hm = jnp.where(mine, 0.125, 0.0).astype(bf16)
+    return t, mine, pl.ds(pl.multiple_of(t * 128, 128), 128)
+
+
+def group_fwd(g, qk, k2, v2, bias, ctx, lse):
     for i in range(2):
         rows, n = pl.ds(256 * i, 256), 256 * (i + 1)
-        s = mm(qk[rows, col] * hm, k2[g, pl.ds(0, n)], NT) + bias[rows, pl.ds(0, n)].astype(f32)
-        m = jnp.max(s, axis=1, keepdims=True)
-        p = jnp.exp(s - m)
-        l = jnp.sum(p, axis=1, keepdims=True)
-        o = mm((p * (1.0 / l)).astype(bf16), v2[g, pl.ds(0, n)])
-        ctx[rows, col] = jnp.where(mine, o, ctx[rows, col].astype(f32)).astype(bf16)
-        lse[rows] = jnp.where(lanes() == h, m + jnp.log(l), lse[rows])
-
-
-def head_bwd(h, qk, k2, v2, bias, lse, dctx, dq, dk, dv):
-    t, g, mine, col = head_at(h)
-    hm = jnp.where(mine, 0.125, 0.0).astype(bf16)
-    om = jnp.where(mine, 1.0, 0.0).astype(bf16)
+        sums = lse[rows]
+        for h in (3 * g, 3 * g + 1, 3 * g + 2):
+            t, mine, col = head_at(h)
+            hm = jnp.where(mine, 0.125, 0.0).astype(bf16)
+            s = mm(qk[rows, col] * hm, k2[g, pl.ds(0, n)], NT) + bias[rows, pl.ds(0, n)].astype(f32)
+            m = jnp.max(s, axis=1, keepdims=True)
+            p = jnp.exp(s - m)
+            l = jnp.sum(p, axis=1, keepdims=True)
+            o = mm((p * (1.0 / l)).astype(bf16), v2[g, pl.ds(0, n)])
+            ctx[rows, col] = jnp.where(mine, o, ctx[rows, col].astype(f32)).astype(bf16)
+            sums = jnp.where(lanes() == h, m + jnp.log(l), sums)
+        lse[rows] = sums
+
+
+def group_bwd(g, qk, k2, v2, bias, lse, dctx, dq, dk, dv):
     for i in range(2):
         rows, n = pl.ds(256 * i, 256), 256 * (i + 1)
-        qs = qk[rows, col] * hm
-        do = dctx[t // 4, rows, pl.ds(pl.multiple_of((t % 4) * 128, 128), 128)] * om
-        le = jnp.sum(jnp.where(lanes() == h, lse[rows], 0.0), axis=1, keepdims=True)
-        s = mm(qs, k2[g, pl.ds(0, n)], NT) + bias[rows, pl.ds(0, n)].astype(f32)
-        p = jnp.exp(s - le)
-        dp = mm(do, v2[g, pl.ds(0, n)], NT)
-        dv[g, pl.ds(0, n)] += mm(p.astype(bf16), do, TN)
-        ds = (p * (dp - jnp.sum(p * dp, axis=1, keepdims=True))).astype(bf16)
-        dk[g, pl.ds(0, n)] += mm(ds, qs, TN)
-        dq[rows, col] = jnp.where(mine, mm(ds, k2[g, pl.ds(0, n)]) * 0.125, dq[rows, col])
+        dk_part, dv_part = 0.0, 0.0
+        for h in (3 * g, 3 * g + 1, 3 * g + 2):
+            t, mine, col = head_at(h)
+            hm = jnp.where(mine, 0.125, 0.0).astype(bf16)
+            om = jnp.where(mine, 1.0, 0.0).astype(bf16)
+            qs = qk[rows, col] * hm
+            do = dctx[t // 4, rows, pl.ds(pl.multiple_of((t % 4) * 128, 128), 128)] * om
+            le = jnp.sum(jnp.where(lanes() == h, lse[rows], 0.0), axis=1, keepdims=True)
+            s = mm(qs, k2[g, pl.ds(0, n)], NT) + bias[rows, pl.ds(0, n)].astype(f32)
+            p = jnp.exp(s - le)
+            dp = mm(do, v2[g, pl.ds(0, n)], NT)
+            dv_part += mm(p.astype(bf16), do, TN)
+            ds = (p * (dp - jnp.sum(p * dp, axis=1, keepdims=True))).astype(bf16)
+            dk_part += mm(ds, qs, TN)
+            dq[rows, col] = jnp.where(mine, mm(ds, k2[g, pl.ds(0, n)]) * 0.125, dq[rows, col])
+        if i == 0:
+            dk[g] = jnp.zeros_like(dk[g])
+            dv[g] = jnp.zeros_like(dv[g])
+        dk[g, pl.ds(0, n)] += dk_part
+        dv[g, pl.ds(0, n)] += dv_part
 
 
 KEYS = [(7, 1), (8, 0), (8, 1), (9, 0), (9, 1)]
@@ -770,9 +843,15 @@
     tl.start()
     cl = pltpu.make_async_copy(cotT, boT, lsem.at[1])
     cl.start()
-    pl.semaphore_wait(bar, 6)
+    pl.semaphore_wait(bar, len(w.peers()))
+
+    def summed(u):
+        if u < 5:
+            return SM.at[u]
+        return SO.at[u - 5] if u < 7 else SO.at[2, :, :, slice(*((0, 128), (128, 240))[u - 7])]
+
     ga = Gather(w, own, W, sems[:5])
-    re = Reduce(w, lambda u: SM.at[u] if u < 5 else SO.at[u - 5], RX3, RY3, RX, RY, RZ, FIN, sems[5:])
+    re = Reduce(w, summed, RX3, RY3, RX, RY, RZ, FIN, sems[5:])
     live, local = {}, {}
 
     def psend(i, src, dst):
@@ -814,8 +893,6 @@
         lse[...] = jnp.zeros_like(lse)
         acc[...] = jnp.zeros_like(acc)
         dacc[...] = jnp.zeros_like(dacc)
-        dk[...] = jnp.zeros_like(dk)
-        dv[...] = jnp.zeros_like(dv)
         tl.wait()
         cl.wait()
         mid[...] = jnp.swapaxes(tgT[...], 0, 1).astype(f32)
@@ -1042,18 +1119,18 @@
             else:
                 (ga if name[0] == "g" else re).step(name, at)
 
-    def after(i, parts, at=None):
+    def after(i, parts):
         for n, part in enumerate(parts):
             if part:
-                pl.when(i == (n if at is None else at(n)))(lambda part=part: run(part))
-
-    def heads(one_head, parts):
-        def turn(h, _):
-            one_head(h)
-            after(h, parts, lambda n: 3 * n + 2)
+                pl.when(i == n)(lambda part=part: run(part))
+
+    def heads(group, parts):
+        def turn(g, _):
+            group(g)
+            after(g, parts)
             return 0
 
-        lax.fori_loop(0, 15, turn, 0)
+        lax.fori_loop(0, 5, turn, 0)
 
     def unit(j, _):
         F(j)
@@ -1063,11 +1140,11 @@
         return 0
 
     run(PARTS["start"])
-    heads(lambda h: head_fwd(h, qk, k2, v2, bias, da, lse), PARTS["H"])
+    heads(lambda g: group_fwd(g, qk, k2, v2, bias, da, lse), PARTS["H"])
     run(PARTS["A3"])
     lax.fori_loop(0, 5, unit, 0)
     run(PARTS["B1"])
-    heads(lambda h: head_bwd(h, qk, k2, v2, bias, lse, hid, acc, dk, dv), PARTS["K"])
+    heads(lambda g: group_bwd(g, qk, k2, v2, bias, lse, hid, acc, dk, dv), PARTS["K"])
     run(PARTS["D1"])
     for i in list(live):
         psent(i)
@@ -1103,8 +1180,8 @@
             V(5, 4, 4, 368, 128), V(3, 4, 4, 240, 128),
             V(2, ROWS, 128), V(2, ROWS, 128), V(4, ROWS, 128), V(4, ROWS, 128), V(3, ROWS, 128),
             D((8,)), D((17,)), D((17,)),
-            D((8, 11)), D((8, 3)), D((8, 2)), D((8, 2)), D((8, 4)),
-            D((8, 17)), D((8, 2)), D((8, 4)), D((8, 3)), D((8, 8)), D((8,)),
+            D((9, 11)), D((9, 3)), D((9, 2)), D((9, 2)), D((9, 4)),
+            D((9, 18)), D((9, 2)), D((9, 4)), D((9, 4)), D((9, 8)), D((9,)),
         ],
         compiler_params=pltpu.CompilerParams(
             collective_id=0, has_side_effects=True, vmem_limit_bytes=67043328
@@ -1116,88 +1193,91 @@
 PARTS = {
     "start": [
         ("g0", 0), ("g0", 1), ("g0", 2), ("g0", 3), ("A0", None), ("g1", 0), ("g0", 4), ("g1", 1), ("g0", 5),
-        ("g2a", 0), ("g2b", 0), ("g1", 2), ("g0", 6), ("g2a", 1), ("g2b", 1), ("g3", 0), ("g4", 0),
-        ("g2a", 2), ("g2b", 2), ("g1", 3), ("g0", 7), ("g3", 1), ("g4", 1), ("LQ", None), ("g3", 2),
-        ("g4", 2), ("LO", None), ("g1", 4), ("A1", None), ("g2a", 3), ("g2b", 3),
+        ("g2a", 0), ("g2b", 0), ("g1", 2), ("g2a", 1), ("g2b", 1), ("g0", 6), ("g3", 0), ("g4", 0), ("g1", 3),
+        ("g0", 7), ("g2a", 2), ("g2b", 2), ("g3", 1), ("g4", 1), ("g2a", 3), ("g2b", 3), ("g1", 4), ("g0", 8),
+        ("g3", 2), ("g4", 2), ("LQ", None), ("g3", 3), ("g4", 3), ("LO", None), ("g1", 5), ("A1", None),
+        ("g2a", 4), ("g2b", 4),
     ],
     "H": [
         [
-            ("g2a", 4), ("g2b", 4), ("g1", 5),
-        ],
-        [
-            ("g3", 3),
-        ],
-        [
-            ("g3", 4), ("g1", 6), ("g4", 3), ("L", 0),
-        ],
-        [
-            ("g4", 4),
-        ],
-        [
-            ("g2a", 5), ("g2b", 5),
+            ("g2a", 5), ("g2b", 5), ("g1", 6),
+        ],
+        [],
+        [
+            ("g3", 4), ("g1", 7),
+        ],
+        [
+            ("g3", 5), ("g4", 4), ("L", 0),
+        ],
+        [
+            ("g2a", 6), ("g2b", 6), ("g4", 5),
         ],
     ],
     "A3": [
-        ("A3", None), ("L", 1), ("g1", 7),
+        ("A3", None), ("L", 1), ("g1", 8),
     ],
     "F": [
         [
-            ("g3", 5), ("g2a", 6), ("g2b", 6),
-        ],
-        [
             ("g3", 6), ("g2a", 7), ("g2b", 7),
         ],
+        [
+            ("g3", 7), ("g2a", 8), ("g2b", 8),
+        ],
+        [
+            ("g3", 8),
+        ],
         [],
-        [
-            ("c3", 0), ("c2a", 1), ("c2b", 1), ("g4", 7), ("L", 4),
-        ],
         [
             ("c2a", 2), ("c2b", 2),
         ],
     ],
     "R": [
         [
-            ("c1", 0), ("g4", 5), ("L", 2),
-        ],
-        [
-            ("c2a", 0), ("c2b", 0), ("c1", 1), ("g4", 6), ("L", 3),
-        ],
-        [
-            ("g3", 7), ("c1", 2),
-        ],
-        [
-            ("c1", 3),
-        ],
-        [
-            ("c4", 0), ("c1", 4),
+            ("z1", 0), ("g4", 6), ("L", 2),
+        ],
+        [
+            ("c1", 1), ("g4", 7), ("L", 3),
+        ],
+        [
+            ("c2a", 1), ("c2b", 1), ("c1", 2), ("g4", 8), ("L", 4),
+        ],
+        [
+            ("c3", 1), ("c1", 3),
+        ],
+        [
+            ("z2", 0), ("c1", 4),
         ],
     ],
     "B1": [
-        ("B1", None), ("c3", 1), ("B2", None), ("c2a", 3), ("c2b", 3), ("c1", 5),
+        ("B1", None), ("c2a", 3), ("c2b", 3), ("B2", None), ("c1", 5),
     ],
     "K": [
+        [
+            ("c4", 1), ("c3", 2), ("z3a", 0), ("z3b", 0),
+        ],
+        [
+            ("c2a", 4), ("c2b", 4),
+        ],
         [],
         [
-            ("c4", 1), ("c5a", 0), ("c3", 2),
-        ],
-        [
-            ("c5b", 0), ("c2b", 4), ("c2a", 4),
-        ],
-        [],
-        [
             ("c4", 2), ("c3", 3),
+        ],
+        [
+            ("c2a", 5), ("c2b", 5),
         ],
     ],
     "D1": [
-        ("D1", None), ("c2a", 5), ("c2b", 5), ("D2", None), ("c5a", 1), ("c1", 6), ("D3", None), ("c6", 0),
-        ("c5b", 1), ("D4", None), ("c1", 7), ("c4", 3), ("c3", 4), ("c5a", 2), ("c7", 0), ("c5b", 2),
-        ("c3", 5), ("c2b", 6), ("c2a", 6), ("c6", 1), ("c7", 1), ("c4", 4), ("c2b", 7), ("c2a", 7),
-        ("c5a", 3), ("c4", 5), ("c5b", 3), ("c6", 2), ("c7", 2), ("c3", 6), ("c5a", 4), ("c5b", 4), ("c3", 7),
-        ("c5a", 5), ("c6", 3), ("c7", 3), ("c5b", 5), ("c6", 4), ("c4", 6), ("c7", 4), ("c6", 5), ("c7", 5),
-        ("c5a", 6), ("c5b", 6), ("c4", 7), ("c6", 6), ("c7", 6), ("c5a", 7), ("c5b", 7), ("c6", 7), ("c7", 7),
+        ("D1", None), ("c5a", 1), ("c5b", 1), ("D3", None), ("z4", 0), ("D2", None), ("c5a", 2), ("c5b", 2),
+        ("c4", 3), ("c3", 4), ("c1", 6), ("D4", None), ("c6", 1), ("c3", 5), ("c1", 7), ("c1", 8), ("c7", 1),
+        ("c5a", 0), ("c5b", 0), ("c6", 2), ("c7", 2), ("c5a", 3), ("c5b", 3), ("c2b", 6), ("c2a", 6),
+        ("c4", 4), ("c2b", 7), ("c2a", 7), ("c2b", 8), ("c2a", 8), ("c4", 5), ("c6", 0), ("c6", 3), ("c7", 0),
+        ("c7", 3), ("c3", 6), ("c5a", 4), ("c5b", 4), ("c3", 7), ("c3", 8), ("c5a", 5), ("c5b", 5), ("c6", 4),
+        ("c7", 4), ("c4", 6), ("c6", 5), ("c7", 5), ("c4", 7), ("c5a", 6), ("c5b", 6), ("c4", 8), ("c6", 6),
+        ("c5a", 7), ("c5b", 7), ("c7", 6), ("c6", 7), ("c7", 7), ("c5a", 8), ("c5b", 8), ("c6", 8), ("c7", 8),
     ],
 }
 
+DIAGONAL = (6, 7, 8)
 
 def on_device(tokens, sequence_ids, cotangent, norm_gains, qkv_weight, out_weight, gate_up_weight, down_weight, *moments):
     weights = (norm_gains, qkv_weight, out_weight, gate_up_weight, down_weight)

time: 255 us -> 244 us (0.957)
  Pallas kernels: 249 us -> 239 us
    pallas_call x1, Pallas kernels: 211 us -> 203 us  [layer(): pl.pallas_call(layer_kernel, name='layer', out_shape=[S((960, 512), bf16)...]
where the time goes in v1:
time: 244 us; the launch traced here: 243 us
  Pallas kernels  239 us (98%)
  local copies, waits for them, and re-layouts  2.49 us (1%)
    pallas_call x1, Pallas kernels, layer(): pl.pallas_call(layer_kernel, name='layer', out_shape=[S((960, 512), bf16)...  203 us
    pallas_call x1, Pallas kernels, adam(): pl.pallas_call(adam_kernel, name='adam', grid=(8,), out_shape=shapes, in_...  27.6 us
    pallas_call x1, Pallas kernels, pack(): pl.pallas_call(pack_kernel, name='pack', grid=(8,), out_shape=jax.ShapeDt...  8.61 us

profile of v1, /device:TPU:0, one launch (start us, length us, event | category | flops | bytes accessed | tf_op | source)
XLA Modules:
  0.0 242.7 jit_solution(16598857964622554209)
XLA Ops:
  0.7 0.5 fusion.2.freq
  1.2 8.6 %pack.1.own = bf16[8,2560,128]{2,1,0:T(8,128)(2,1)} custom-call(f32[2,240]{1,0:T(2,128)} %refs_0_.1, f32[240,1600]{1,0:T(8,128)} %refs_1_.1, f32[240,960]{1,0:T(8,128)} %refs_2_.1, f32[240,5120]{1,0:T(8,128)} %refs_3_.1, f32[960,640]{1,0:T(8,128)} %bitcast.12), custom_call_target="tpu_custom_call" | custom-call | tf_op jit(solution)/shard_map/pack/pallas_call | solution.py:411
  9.8 202.8 %layer.1 = (bf16[960,512]{1,0:T(8,128)(2,1)}, bf16[960,512]{1,0:T(8,128)(2,1)}, bf16[8,2560,128]{2,1,0:T(8,128)(2,1)}, bf16[8,3,2560,128]{3,2,1,0:T(8,128)(2,1)}...) custom-call(bf16[960,512]{1,0:T(8,128)(2,1)} %bitcast.16, bf16[960,512]{1,0:T(8,128)(2,1)} %bitcast.17, ...), custom_call_target="tpu_custom_call" | custom-call | tf_op jit(solution)/shard_map/layer/pallas_call | solution.py:1164
  212.6 0.0 copy-start.1
  212.6 27.6 %adam.1 = (f32[2,240]{1,0:T(2,128)}, f32[240,1600]{1,0:T(8,128)}, f32[240,960]{1,0:T(8,128)}, f32[240,5120]{1,0:T(8,128)}, f32[960,640]{1,0:T(8,128)}, /*index=5...) custom-call(bf16[8,2560,128]{2,1,0:T(8,128)(2,1)} %get-tuple-element, ...), custom_call_target="tpu_custom_call" | custom-call | tf_op jit(solution)/shard_map/adam/pallas_call | solution.py:468
  240.2 0.0 copy-start
  240.2 0.0 copy-done.1
  240.2 0.9 copy.42
  241.2 0.6 copy-done
  241.8 0.9 copy.43
Async XLA Ops:
  212.6 27.7 %copy-start.1 = (bf16[960,512]{1,0:T(8,128)(2,1)S(1)}, bf16[960,512]{1,0:T(8,128)(2,1)}, u32[]{:S(2)}) copy-start(bf16[960,512]{1,0:T(8,128)(2,1)} %get-tuple-element.45) | copy-start | bytes 2949124
  240.2 1.6 copy-start

commit v2 on v1

--- a/solution.py
+++ b/solution.py
@@ -389,35 +389,6 @@
     ]
 
 
-def pack_kernel(gains, qkv, out, gu, dnT, own):
-    k = pl.program_id(0)
-    own[0, 0:240] = qkv[:, 0:128].astype(bf16)
-    own[0, 240:480] = qkv[:, 128:256].astype(bf16)
-
-    @pl.when(k % 4 == 3)
-    def _():
-        row = jnp.where(k == 3, gains[0:1], gains[1:2])
-        tile = jnp.where(lax.broadcasted_iota(jnp.int32, (128, 240), 0) == 0, row, 0.0)
-        own[0, 240:480] = jnp.swapaxes(tile, 0, 1).astype(bf16)
-
-    own[0, 480:720] = jnp.where(lanes() < 960 - k * 128, out[...], 0.0).astype(bf16)
-    for j in range(5):
-        own[0, 720 + 368 * j : 960 + 368 * j] = gu[:, j * 128 : (j + 1) * 128].astype(bf16)
-        t = jnp.swapaxes(dnT[:, j * 128 : (j + 1) * 128].astype(bf16), 0, 1)
-        own[0, 960 + 368 * j : 1088 + 368 * j] = jnp.where(lanes() < 960 - k * 128, t.astype(f32), 0.0).astype(bf16)
-
-
-def pack(norm_gains, qkv, out, gu, down):
-    return pl.pallas_call(
-        pack_kernel,
-        name="pack",
-        grid=(8,),
-        out_shape=jax.ShapeDtypeStruct((8, ROWS, 128), bf16),
-        in_specs=param_specs(),
-        out_specs=pl.BlockSpec((1, ROWS, 128), lambda k: (k, 0, 0)),
-    )(norm_gains, qkv, out, gu, down.T)
-
-
 def adam_kernel(FIN, *refs):
     weight, first, second = refs[0:5], refs[5:10], refs[10:15]
     grad, delta, first_new, second_new = refs[15:20], refs[20:25], refs[25:30], refs[30:35]
@@ -522,7 +493,8 @@
 
     def step(g, name, u):
         getattr(g, name)(u)
-        g.ran.append((name, u))
+        if name != "g0":
+            g.ran.append((name, u))
 
     def finish(g):
         g.waiting = True
@@ -543,8 +515,7 @@
     def g0(g, u):
         r0, n, h = GATHER_UNITS[u]
         for d in range(3):
-            src = g.own.at[g.w.k, pl.ds(r0, n)]
-            g.send(u, d, src, g.W.at[g.w.k, d, pl.ds(r0, n)], g.rz.at[u, d], g.w.zn[d])
+            g.send(u, d, g.own(u, g.w.k), g.W.at[g.w.k, d, pl.ds(r0, n)], g.rz.at[u, d], g.w.zn[d])
 
     def g1(g, u):
         r0, n, h = GATHER_UNITS[u]
@@ -731,20 +702,20 @@
 
 def load_unit(w, own, W, dst, sem, u0, n, row0=0, halves=False):
     def block(k, _):
-        def one(r, view, c0):
+        def one(r, s, view, c0):
             def put(src, zs):
                 rows = pl.ds(pl.multiple_of(row0 + zs * n, 16), n)
                 pltpu.make_async_copy(src, view.at[rows, pl.ds(pl.multiple_of(c0, 128), 128)], sem).start()
 
-            put(own.at[k, pl.ds(r, n)], w.z)
+            put(own(k, s), w.z)
             for d in range(3):
                 put(W.at[k, d, pl.ds(r, n)], (w.z + 3 - d) % 4)
 
         if halves:
             for s in range(2):
-                one(u0 + s * n, dst.at[k // 4], (k % 4) * 256 + s * 128)
+                one(u0 + s * n, s, dst.at[k // 4], (k % 4) * 256 + s * 128)
         else:
-            one(u0, dst, k * 128)
+            one(u0, 0, dst, k * 128)
         return 0
 
     lax.fori_loop(0, 8, block, 0)
@@ -827,18 +798,39 @@
 
 
 def layer_kernel(
-    tokT, cotT, freq, ids, own,
+    tokT, cotT, freq, ids, norm_gains, qkv, out, gate_up, downT,
     boT, tgT, FIN, W, n1H, ctxH,
     cot, cos, sin, qk, k2, v2, lse, mid, n2, gains,
     wg, wd, bias, n2T, n2pT, cpT, dypp, hid, dgu, hidp, dgup, da, acc, dacc, dk, dv, gcol, gcolp,
-    SM, SO, RX3, RY3, RX, RY, RZ,
-    lsem, ps, pr, *sems,
+    SM, SO, RX3, RY3, RX, RY, RZ, stage,
+    lsem, wsem, ps, pr, *sems,
 ):
     w = Where()
     c = w.c
     bar = pltpu.get_barrier_semaphore()
     for p in w.peers():
         pl.semaphore_signal(bar, inc=1, device_id=p, device_id_type=MESH)
+    loads = {}
+
+    def fetch(name, *pairs):
+        loads[name] = [pltpu.make_async_copy(src, dst, wsem.at[len(loads)]) for src, dst in pairs]
+        for cp in loads[name]:
+            cp.start()
+
+    def fetch_unit(j):
+        rows = slice(256 * (j % 2), 256 * (j % 2) + 240)
+        cols = [(gate_up.at[:, k * 640 + j * 128 : k * 640 + (j + 1) * 128], acc.at[rows, k * 128 : (k + 1) * 128]) for k in range(8)]
+        for k in range(8):
+            pltpu.make_async_copy(*cols[k], wsem.at[2 + j]).start()
+        part = downT.at[:, j * 128 : (j + 1) * 128]
+        turned = (dk, dv)[j % 2]
+        pltpu.make_async_copy(part.at[0:512], turned.at[0], wsem.at[7 + j]).start()
+        pltpu.make_async_copy(part.at[512:960], turned.at[1, 0:448], wsem.at[12 + j]).start()
+
+    fetch("qkv", (qkv, stage))
+    fetch("out", (out, dacc.at[0:240]))
+    fetch_unit(0)
+    fetch_unit(1)
     tl = pltpu.make_async_copy(tokT, tgT, lsem.at[0])
     tl.start()
     cl = pltpu.make_async_copy(cotT, boT, lsem.at[1])
@@ -850,7 +842,13 @@
             return SM.at[u]
         return SO.at[u - 5] if u < 7 else SO.at[2, :, :, slice(*((0, 128), (128, 240))[u - 7])]
 
-    ga = Gather(w, own, W, sems[:5])
+    def held(u, k):
+        at = (k // 4, k % 4)
+        if u >= 4:
+            return SM.at[u - 4, *at]
+        return (SO.at[1, *at, 0:128], SO.at[1, *at, 128:240], SO.at[2, *at], SO.at[0, *at])[u]
+
+    ga = Gather(w, held, W, sems[:5])
     re = Reduce(w, summed, RX3, RY3, RX, RY, RZ, FIN, sems[5:])
     live, local = {}, {}
 
@@ -875,6 +873,47 @@
     other = pl.ds(pl.multiple_of((1 - c) * 512, 512), 512)
     mine = pl.ds(pl.multiple_of(c * 512, 512), 512)
     half_rows = [pl.ds(256 * i, 256) for i in range(2)]
+
+    zero = jnp.zeros((240, 128), bf16)
+
+    def PQ():
+        loads["qkv"][0].wait()
+        for t in range(13):
+            k, sub = (t // 2, t % 2) if t < 6 else (4 + (t - 6) // 2, (t - 6) % 2)
+            tile = SO.at[1 + sub, k // 4, k % 4]
+            if t < 12:
+                tile[...] = stage[:, t * 128 : (t + 1) * 128].astype(bf16)
+            else:
+                tile[...] = zero
+                tile[:, 0:64] = stage[:, 1536:1600].astype(bf16)
+        SO[1, 0, 3] = zero
+        for i in range(2):
+            at = lax.broadcasted_iota(jnp.int32, (128, 240), 0) == 0
+            tile = jnp.where(at, norm_gains[i : i + 1], 0.0)
+            SO[2, i, 3] = jnp.swapaxes(tile, 0, 1).astype(bf16)
+
+    def PO():
+        loads["out"][0].wait()
+        SO[0, 1, 3] = zero
+        for k in range(8):
+            width = 128 if k < 7 else 64
+            SO[0, k // 4, k % 4, :, 0:width] = dacc[0:240, k * 128 : k * 128 + width].astype(bf16)
+
+    def PM(j):
+        rows = slice(256 * (j % 2), 256 * (j % 2) + 240)
+        turned = (dk, dv)[j % 2]
+        view = acc.at[rows]
+        pltpu.make_async_copy(view, view, wsem.at[2 + j]).wait()
+        for i, part in enumerate((turned.at[0], turned.at[1, 0:448])):
+            pltpu.make_async_copy(part, part, wsem.at[7 + 5 * i + j]).wait()
+        SM[j, 1, 3, 240:368] = jnp.zeros((128, 128), bf16)
+        for k in range(8):
+            width = 128 if k < 7 else 64
+            SM[j, k // 4, k % 4, 0:240] = acc[rows, k * 128 : (k + 1) * 128].astype(bf16)
+            block = turned[k // 4, (k % 4) * 128 : (k % 4) * 128 + width].astype(bf16)
+            SM[j, k // 4, k % 4, 240:368, 0:width] = jnp.swapaxes(block, 0, 1)
+        if j + 2 < 5:
+            fetch_unit(j + 2)
 
     def A0():
         seq = ids[...].astype(f32)
@@ -891,8 +930,6 @@
             cos[pl.ds(256 * i, 256)] = jnp.cos(angle)
             sin[pl.ds(256 * i, 256)] = jnp.where((lanes() % 64) < 32, -1.0, 1.0) * jnp.sin(angle)
         lse[...] = jnp.zeros_like(lse)
-        acc[...] = jnp.zeros_like(acc)
-        dacc[...] = jnp.zeros_like(dacc)
         tl.wait()
         cl.wait()
         mid[...] = jnp.swapaxes(tgT[...], 0, 1).astype(f32)
@@ -900,13 +937,13 @@
         cot[:, 0:960] = jnp.swapaxes(boT[...], 0, 1)
 
     def LQ():
-        load_unit(w, own, W, wg, lsem.at[0], 0, 240, halves=True)
+        load_unit(w, lambda k, s: SO.at[1 + s, k // 4, k % 4], W, wg, lsem.at[0], 0, 240, halves=True)
 
     def wait_q():
         pltpu.make_async_copy(wg, wg, lsem.at[0]).wait()
 
     def LO():
-        load_unit(w, own, W, wd, lsem.at[1], 480, 240)
+        load_unit(w, lambda k, s: SO.at[0, k // 4, k % 4], W, wd, lsem.at[1], 480, 240)
 
     def wait_o():
         view = wd.at[pl.ds(0, 960)]
@@ -914,6 +951,8 @@
 
     def A1():
         wait_q()
+        acc[...] = jnp.zeros_like(acc)
+        dacc[...] = jnp.zeros_like(dacc)
         gains[...] = jnp.zeros_like(gains)
         gains[0:1] = gain_row(wg[0, :, 896:1024])
         gains[1:2] = gain_row(wg[1, :, 896:1024])
@@ -952,8 +991,11 @@
         return pl.ds(pl.multiple_of(((j + 2) % 3) * 512, 512), 512)
 
     def L(j):
-        load_unit(w, own, W, wg.at[j % 2], lsem.at[4 + j % 2], 720 + 368 * j, 240)
-        load_unit(w, own, W, wd, lsem.at[6 + j % 2], 960 + 368 * j, 128, row0=((j + 2) % 3) * 512)
+        def rows(a, b):
+            return lambda k, s: SM.at[j, k // 4, k % 4, a:b]
+
+        load_unit(w, rows(0, 240), W, wg.at[j % 2], lsem.at[4 + j % 2], 720 + 368 * j, 240)
+        load_unit(w, rows(240, 368), W, wd, lsem.at[6 + j % 2], 960 + 368 * j, 128, row0=((j + 2) % 3) * 512)
 
     def sends(j):
         b = j % 2
@@ -1110,7 +1152,7 @@
         pgot(16, gcolp)
         qgrad(1)
 
-    steps = dict(A0=A0, LQ=LQ, A1=A1, LO=LO, A3=A3, L=L, B1=B1, B2=B2, D1=D1, D2=D2, D3=D3, D4=D4)
+    steps = dict(PQ=PQ, PO=PO, PM=PM, A0=A0, LQ=LQ, A1=A1, LO=LO, A3=A3, L=L, B1=B1, B2=B2, D1=D1, D2=D2, D3=D3, D4=D4)
 
     def run(part):
         for name, at in part:
@@ -1142,6 +1184,10 @@
     run(PARTS["start"])
     heads(lambda g: group_fwd(g, qk, k2, v2, bias, da, lse), PARTS["H"])
     run(PARTS["A3"])
+    ga.waiting = True
+    for u in range(len(GATHER_UNITS)):
+        ga.g0(u)
+    ga.waiting = False
     lax.fori_loop(0, 5, unit, 0)
     run(PARTS["B1"])
     heads(lambda g: group_bwd(g, qk, k2, v2, bias, lse, hid, acc, dk, dv), PARTS["K"])
@@ -1152,7 +1198,7 @@
     re.finish()
 
 
-def layer(tok, cot, ids, own):
+def layer(tok, cot, ids, weights):
     freq = ROPE_BASE ** (-2.0 * (jnp.arange(128) % 32).astype(f32) / HEAD)
     S, D = jax.ShapeDtypeStruct, pltpu.SemaphoreType.DMA
 
@@ -1168,7 +1214,7 @@
             S((960, 512), bf16), S((960, 512), bf16), S((8, ROWS, 128), bf16),
             S((8, 3, ROWS, 128), bf16), S((960, 512), bf16), S((960, 512), bf16),
         ],
-        in_specs=[hb, hb, vm, vm, hb],
+        in_specs=[hb, hb, vm, vm, vm, hb, hb, hb, hb],
         out_specs=[vm, vm, hb, hb, hb, hb],
         scratch_shapes=[
             V(512, 1024), V(512, 128, dt=f32), V(512, 128, dt=f32), V(512, 1280), V(5, 512, 128), V(5, 512, 128), V(512, 128, dt=f32), V(512, 960, dt=f32),
@@ -1178,25 +1224,26 @@
             V(512, 1024, dt=f32), V(512, 960, dt=f32), V(5, 512, 128, dt=f32), V(5, 512, 128, dt=f32),
             V(2, 960, 128), V(960, 128),
             V(5, 4, 4, 368, 128), V(3, 4, 4, 240, 128),
-            V(2, ROWS, 128), V(2, ROWS, 128), V(4, ROWS, 128), V(4, ROWS, 128), V(3, ROWS, 128),
-            D((8,)), D((17,)), D((17,)),
+            V(2, ROWS, 128), V(2, ROWS, 128), V(4, ROWS, 128), V(4, ROWS, 128), V(3, ROWS, 128), V(240, 1600, dt=f32),
+            D((8,)), D((17,)), D((17,)), D((17,)),
             D((9, 11)), D((9, 3)), D((9, 2)), D((9, 2)), D((9, 4)),
             D((9, 18)), D((9, 2)), D((9, 4)), D((9, 4)), D((9, 8)), D((9,)),
         ],
         compiler_params=pltpu.CompilerParams(
             collective_id=0, has_side_effects=True, vmem_limit_bytes=67043328
         ),
-    )(tok.T, cot.T, freq[None, :], ids[None, :], own)
+    )(tok.T, cot.T, freq[None, :], ids[None, :], *weights[:4], weights[4].T)
     return outs[:3]
 
 
 PARTS = {
     "start": [
-        ("g0", 0), ("g0", 1), ("g0", 2), ("g0", 3), ("A0", None), ("g1", 0), ("g0", 4), ("g1", 1), ("g0", 5),
-        ("g2a", 0), ("g2b", 0), ("g1", 2), ("g2a", 1), ("g2b", 1), ("g0", 6), ("g3", 0), ("g4", 0), ("g1", 3),
-        ("g0", 7), ("g2a", 2), ("g2b", 2), ("g3", 1), ("g4", 1), ("g2a", 3), ("g2b", 3), ("g1", 4), ("g0", 8),
-        ("g3", 2), ("g4", 2), ("LQ", None), ("g3", 3), ("g4", 3), ("LO", None), ("g1", 5), ("A1", None),
-        ("g2a", 4), ("g2b", 4),
+        ("PQ", None), ("g0", 0), ("g0", 1), ("g0", 2), ("PO", None), ("g0", 3), ("PM", 0), ("PM", 1),
+        ("A0", None), ("PM", 2), ("g1", 0), ("g0", 4), ("PM", 3), ("PM", 4), ("g1", 1), ("g0", 5), ("g2a", 0),
+        ("g2b", 0), ("g1", 2), ("g2a", 1), ("g2b", 1), ("g0", 6), ("g3", 0), ("g4", 0), ("g1", 3), ("g0", 7),
+        ("g2a", 2), ("g2b", 2), ("g3", 1), ("g4", 1), ("g2a", 3), ("g2b", 3), ("g1", 4), ("g0", 8), ("g3", 2),
+        ("g4", 2), ("LQ", None), ("g3", 3), ("g4", 3), ("LO", None), ("g1", 5), ("A1", None), ("g2a", 4),
+        ("g2b", 4),
     ],
     "H": [
         [
@@ -1281,7 +1328,7 @@
 
 def on_device(tokens, sequence_ids, cotangent, norm_gains, qkv_weight, out_weight, gate_up_weight, down_weight, *moments):
     weights = (norm_gains, qkv_weight, out_weight, gate_up_weight, down_weight)
-    block_out, tokens_grad, packed = layer(tokens, cotangent, sequence_ids, pack(*weights))
+    block_out, tokens_grad, packed = layer(tokens, cotangent, sequence_ids, weights)
     return (block_out.T, tokens_grad.T, *adam(packed, weights, moments))
 
 

time: 244 us -> 237 us (0.971)
  Pallas kernels: 239 us -> 230 us
    pallas_call x1 -> x0, Pallas kernels: 8.61 us -> none  [pack(): pl.pallas_call(pack_kernel, name='pack', grid=(8,), out_shape=jax.ShapeDt...]
where the time goes in v2:
time: 237 us; the launch traced here: 233 us
  Pallas kernels  230 us (97%)
  local copies, waits for them, and re-layouts  2.49 us (1%)
    pallas_call x1, Pallas kernels, layer(): pl.pallas_call(layer_kernel, name='layer', out_shape=[S((960, 512), bf16)...  202 us
    pallas_call x1, Pallas kernels, adam(): pl.pallas_call(adam_kernel, name='adam', grid=(8,), out_shape=shapes, in_...  27.6 us

profile of v2, /device:TPU:0, one launch (start us, length us, event | category | flops | bytes accessed | tf_op | source)
XLA Modules:
  0.0 233.5 jit_solution(8058906203316829725)
XLA Ops:
  0.7 0.5 fusion.2.freq
  1.2 202.1 %layer.1 = (bf16[960,512]{1,0:T(8,128)(2,1)}, bf16[960,512]{1,0:T(8,128)(2,1)}, bf16[8,2560,128]{2,1,0:T(8,128)(2,1)}, bf16[8,3,2560,128]{3,2,1,0:T(8,128)(2,1)}...) custom-call(bf16[960,512]{1,0:T(8,128)(2,1)} %bitcast.16, bf16[960,512]{1,0:T(8,128)(2,1)} %bitcast.17, ...), custom_call_target="tpu_custom_call" | custom-call | tf_op jit(solution)/shard_map/layer/pallas_call | solution.py:1210
  203.3 0.0 copy-start.1
  203.3 27.6 %adam.1 = (f32[2,240]{1,0:T(2,128)}, f32[240,1600]{1,0:T(8,128)}, f32[240,960]{1,0:T(8,128)}, f32[240,5120]{1,0:T(8,128)}, f32[960,640]{1,0:T(8,128)}, /*index=5...) custom-call(bf16[8,2560,128]{2,1,0:T(8,128)(2,1)} %get-tuple-element, ...), custom_call_target="tpu_custom_call" | custom-call | tf_op jit(solution)/shard_map/adam/pallas_call | solution.py:439
  231.0 0.0 copy-start
  231.0 0.0 copy-done.1
  231.0 0.9 copy.42
  232.0 0.6 copy-done
  232.5 0.9 copy.43
Async XLA Ops:
  203.3 27.7 %copy-start.1 = (bf16[960,512]{1,0:T(8,128)(2,1)S(1)}, bf16[960,512]{1,0:T(8,128)(2,1)}, u32[]{:S(2)}) copy-start(bf16[960,512]{1,0:T(8,128)(2,1)} %get-tuple-element.45) | copy-start | bytes 2949124
  231.0 1.6 copy-start

commit v3 on v2

--- a/solution.py
+++ b/solution.py
@@ -514,13 +514,34 @@
 
     def g0(g, u):
         r0, n, h = GATHER_UNITS[u]
-        for d in range(3):
+
+        def out(d):
             g.send(u, d, g.own(u, g.w.k), g.W.at[g.w.k, d, pl.ds(r0, n)], g.rz.at[u, d], g.w.zn[d])
+
+        pl.when(g.w.z != 3)(lambda: out(0))
+        out(1)
+        pl.when(g.w.z != 0)(lambda: out(2))
+
+    def gr(g, u):
+        r0, n, h = GATHER_UNITS[u]
+        z = g.w.z
+
+        @pl.when((z == 1) | (z == 2))
+        def _():
+            src = g.W.at[g.w.k, 1, pl.ds(r0, n)]
+            g.got(src, g.rz.at[u, 1])
+            d = 2 * (z - 1)
+            g.send(u, 11, src, g.W.at[g.w.k, d, pl.ds(r0, n)], g.rz.at[u, d], {"fsdp": 3 * (z - 1)})
 
     def g1(g, u):
         r0, n, h = GATHER_UNITS[u]
-        for d in range(3):
+
+        def block(d):
             g.got(g.W.at[g.w.k, d, pl.ds(r0, n)], g.rz.at[u, d])
+
+        block(0)
+        pl.when((g.w.z == 0) | (g.w.z == 3))(lambda: block(1))
+        block(2)
         b = g.reg(g.w.k, u)
         g.send(u, 3, b, b, g.rx.at[u, 0], g.w.xn)
         g.send(u, 4, b, b, g.ry.at[u, 0], g.w.yn)
@@ -1226,7 +1247,7 @@
             V(5, 4, 4, 368, 128), V(3, 4, 4, 240, 128),
             V(2, ROWS, 128), V(2, ROWS, 128), V(4, ROWS, 128), V(4, ROWS, 128), V(3, ROWS, 128), V(240, 1600, dt=f32),
             D((8,)), D((17,)), D((17,)), D((17,)),
-            D((9, 11)), D((9, 3)), D((9, 2)), D((9, 2)), D((9, 4)),
+            D((9, 12)), D((9, 3)), D((9, 2)), D((9, 2)), D((9, 4)),
             D((9, 18)), D((9, 2)), D((9, 4)), D((9, 4)), D((9, 8)), D((9,)),
         ],
         compiler_params=pltpu.CompilerParams(
@@ -1238,89 +1259,95 @@
 
 PARTS = {
     "start": [
-        ("PQ", None), ("g0", 0), ("g0", 1), ("g0", 2), ("PO", None), ("g0", 3), ("PM", 0), ("PM", 1),
-        ("A0", None), ("PM", 2), ("g1", 0), ("g0", 4), ("PM", 3), ("PM", 4), ("g1", 1), ("g0", 5), ("g2a", 0),
-        ("g2b", 0), ("g1", 2), ("g2a", 1), ("g2b", 1), ("g0", 6), ("g3", 0), ("g4", 0), ("g1", 3), ("g0", 7),
-        ("g2a", 2), ("g2b", 2), ("g3", 1), ("g4", 1), ("g2a", 3), ("g2b", 3), ("g1", 4), ("g0", 8), ("g3", 2),
-        ("g4", 2), ("LQ", None), ("g3", 3), ("g4", 3), ("LO", None), ("g1", 5), ("A1", None), ("g2a", 4),
-        ("g2b", 4),
+        ("PQ", None), ("g0", 0), ("g0", 1), ("g0", 2), ("PO", None), ("PM", 0), ("PM", 1), ("A0", None),
+        ("gr", 0), ("PM", 2), ("gr", 1), ("PM", 3), ("PM", 4), ("gr", 2), ("g1", 0), ("g0", 3), ("g1", 1),
+        ("g0", 4), ("g1", 2), ("g0", 5), ("g2a", 0), ("g2b", 0), ("gr", 3), ("g2a", 1), ("g2b", 1), ("gr", 4),
+        ("g2a", 2), ("g2b", 2), ("g3", 0), ("g3", 1), ("g4", 0), ("gr", 5), ("g4", 1), ("g1", 3), ("g0", 6),
+        ("g3", 2), ("g1", 4), ("g0", 7), ("g4", 2), ("LQ", None), ("g1", 5), ("g0", 8), ("g2a", 3),
+        ("g2b", 3), ("A1", None), ("gr", 6), ("gr", 7), ("g2a", 4), ("g2b", 4),
     ],
     "H": [
         [
+            ("gr", 8),
+        ],
+        [
             ("g2a", 5), ("g2b", 5), ("g1", 6),
         ],
-        [],
-        [
-            ("g3", 4), ("g1", 7),
-        ],
-        [
-            ("g3", 5), ("g4", 4), ("L", 0),
-        ],
-        [
-            ("g2a", 6), ("g2b", 6), ("g4", 5),
+        [
+            ("g3", 3), ("g1", 7), ("g1", 8),
+        ],
+        [
+            ("g3", 4), ("g4", 3), ("LO", None), ("g3", 5),
+        ],
+        [
+            ("g4", 4), ("L", 0), ("g4", 5),
         ],
     ],
     "A3": [
-        ("A3", None), ("L", 1), ("g1", 8),
+        ("A3", None), ("L", 1), ("g2a", 6), ("g2b", 6),
     ],
     "F": [
         [
-            ("g3", 6), ("g2a", 7), ("g2b", 7),
-        ],
-        [
-            ("g3", 7), ("g2a", 8), ("g2b", 8),
-        ],
-        [
-            ("g3", 8),
-        ],
-        [],
-        [
-            ("c2a", 2), ("c2b", 2),
+            ("g2a", 7), ("g2b", 7),
+        ],
+        [
+            ("g3", 6), ("g2a", 8), ("g2b", 8),
+        ],
+        [
+            ("L", 4), ("c2a", 1), ("c2b", 1),
+        ],
+        [
+            ("c3", 1),
+        ],
+        [
+            ("z2", 0),
         ],
     ],
     "R": [
         [
-            ("z1", 0), ("g4", 6), ("L", 2),
-        ],
-        [
-            ("c1", 1), ("g4", 7), ("L", 3),
-        ],
-        [
-            ("c2a", 1), ("c2b", 1), ("c1", 2), ("g4", 8), ("L", 4),
-        ],
-        [
-            ("c3", 1), ("c1", 3),
-        ],
-        [
-            ("z2", 0), ("c1", 4),
+            ("z1", 0),
+        ],
+        [
+            ("g3", 7), ("c1", 1), ("g4", 6), ("L", 2), ("g4", 7), ("L", 3), ("g3", 8), ("g4", 8),
+        ],
+        [
+            ("c1", 2),
+        ],
+        [
+            ("c2a", 2), ("c2b", 2), ("c1", 3),
+        ],
+        [
+            ("c3", 2), ("c1", 4),
         ],
     ],
     "B1": [
-        ("B1", None), ("c2a", 3), ("c2b", 3), ("B2", None), ("c1", 5),
+        ("B1", None), ("c4", 1), ("c2a", 3), ("c2b", 3), ("B2", None), ("c1", 5),
     ],
     "K": [
         [
-            ("c4", 1), ("c3", 2), ("z3a", 0), ("z3b", 0),
-        ],
-        [
-            ("c2a", 4), ("c2b", 4),
-        ],
-        [],
-        [
-            ("c4", 2), ("c3", 3),
-        ],
-        [
-            ("c2a", 5), ("c2b", 5),
+            ("z3a", 0), ("z3b", 0),
+        ],
+        [
+            ("c4", 2), ("c2a", 4), ("c2b", 4),
+        ],
+        [
+            ("c5a", 1), ("c5b", 1),
+        ],
+        [
+            ("c3", 3), ("c2a", 5), ("c2b", 5),
+        ],
+        [
+            ("z4", 0),
         ],
     ],
     "D1": [
-        ("D1", None), ("c5a", 1), ("c5b", 1), ("D3", None), ("z4", 0), ("D2", None), ("c5a", 2), ("c5b", 2),
-        ("c4", 3), ("c3", 4), ("c1", 6), ("D4", None), ("c6", 1), ("c3", 5), ("c1", 7), ("c1", 8), ("c7", 1),
-        ("c5a", 0), ("c5b", 0), ("c6", 2), ("c7", 2), ("c5a", 3), ("c5b", 3), ("c2b", 6), ("c2a", 6),
-        ("c4", 4), ("c2b", 7), ("c2a", 7), ("c2b", 8), ("c2a", 8), ("c4", 5), ("c6", 0), ("c6", 3), ("c7", 0),
-        ("c7", 3), ("c3", 6), ("c5a", 4), ("c5b", 4), ("c3", 7), ("c3", 8), ("c5a", 5), ("c5b", 5), ("c6", 4),
-        ("c7", 4), ("c4", 6), ("c6", 5), ("c7", 5), ("c4", 7), ("c5a", 6), ("c5b", 6), ("c4", 8), ("c6", 6),
-        ("c5a", 7), ("c5b", 7), ("c7", 6), ("c6", 7), ("c7", 7), ("c5a", 8), ("c5b", 8), ("c6", 8), ("c7", 8),
+        ("D1", None), ("c5a", 2), ("c5b", 2), ("D3", None), ("c3", 4), ("c6", 1), ("c4", 3), ("D2", None),
+        ("c3", 5), ("c1", 6), ("D4", None), ("c5a", 0), ("c5b", 0), ("c6", 2), ("c1", 7), ("c1", 8),
+        ("c7", 1), ("c5a", 3), ("c5b", 3), ("c7", 2), ("c2b", 6), ("c2a", 6), ("c4", 4), ("c6", 0),
+        ("c2b", 7), ("c7", 0), ("c2a", 7), ("c4", 5), ("c2b", 8), ("c2a", 8), ("c6", 3), ("c7", 3), ("c3", 6),
+        ("c5a", 4), ("c5b", 4), ("c3", 7), ("c5a", 5), ("c5b", 5), ("c3", 8), ("c6", 4), ("c7", 4), ("c6", 5),
+        ("c4", 6), ("c7", 5), ("c4", 7), ("c5a", 6), ("c5b", 6), ("c4", 8), ("c6", 6), ("c5a", 7), ("c5b", 7),
+        ("c7", 6), ("c6", 7), ("c7", 7), ("c5a", 8), ("c5b", 8), ("c6", 8), ("c7", 8),
     ],
 }
 

time: 237 us -> 224 us (0.945); the launches traced: 233 us -> 224 us
  Pallas kernels: 230 us -> 220 us
    pallas_call x1, Pallas kernels: 202 us -> 192 us  [layer(): pl.pallas_call(layer_kernel, name='layer', out_shape=[S((960, 512), bf16)...]
where the time goes in v3:
time: 224 us
  Pallas kernels  220 us (98%)
  local copies, waits for them, and re-layouts  2.49 us (1%)
    pallas_call x1, Pallas kernels, layer(): pl.pallas_call(layer_kernel, name='layer', out_shape=[S((960, 512), bf16)...  192 us
    pallas_call x1, Pallas kernels, adam(): pl.pallas_call(adam_kernel, name='adam', grid=(8,), out_shape=shapes, in_...  27.6 us

profile of v3, /device:TPU:0, one launch (start us, length us, event | category | flops | bytes accessed | tf_op | source)
XLA Modules:
  0.0 223.6 jit_solution(7214759574054560465)
XLA Ops:
  0.7 0.5 fusion.2.freq
  1.2 192.2 %layer.1 = (bf16[960,512]{1,0:T(8,128)(2,1)}, bf16[960,512]{1,0:T(8,128)(2,1)}, bf16[8,2560,128]{2,1,0:T(8,128)(2,1)}, bf16[8,3,2560,128]{3,2,1,0:T(8,128)(2,1)}...) custom-call(bf16[960,512]{1,0:T(8,128)(2,1)} %bitcast.16, bf16[960,512]{1,0:T(8,128)(2,1)} %bitcast.17, ...), custom_call_target="tpu_custom_call" | custom-call | tf_op jit(solution)/shard_map/layer/pallas_call | solution.py:1231
  193.4 0.0 copy-start.1
  193.4 27.6 %adam.1 = (f32[2,240]{1,0:T(2,128)}, f32[240,1600]{1,0:T(8,128)}, f32[240,960]{1,0:T(8,128)}, f32[240,5120]{1,0:T(8,128)}, f32[960,640]{1,0:T(8,128)}, /*index=5...) custom-call(bf16[8,2560,128]{2,1,0:T(8,128)(2,1)} %get-tuple-element, ...), custom_call_target="tpu_custom_call" | custom-call | tf_op jit(solution)/shard_map/adam/pallas_call | solution.py:439
  221.1 0.0 copy-start
  221.1 0.0 copy-done.1
  221.1 0.9 copy.42
  222.0 0.6 copy-done
  222.6 0.9 copy.43
Async XLA Ops:
  193.4 27.7 %copy-start.1 = (bf16[960,512]{1,0:T(8,128)(2,1)S(1)}, bf16[960,512]{1,0:T(8,128)(2,1)}, u32[]{:S(2)}) copy-start(bf16[960,512]{1,0:T(8,128)(2,1)} %get-tuple-element.45) | copy-start | bytes 2949124
  221.1 1.6 copy-start

commit v4 on v3

--- a/solution.py
+++ b/solution.py
@@ -1260,11 +1260,11 @@
 PARTS = {
     "start": [
         ("PQ", None), ("g0", 0), ("g0", 1), ("g0", 2), ("PO", None), ("PM", 0), ("PM", 1), ("A0", None),
-        ("gr", 0), ("PM", 2), ("gr", 1), ("PM", 3), ("PM", 4), ("gr", 2), ("g1", 0), ("g0", 3), ("g1", 1),
+        ("gr", 0), ("gr", 1), ("PM", 2), ("PM", 3), ("PM", 4), ("gr", 2), ("g1", 0), ("g0", 3), ("g1", 1),
         ("g0", 4), ("g1", 2), ("g0", 5), ("g2a", 0), ("g2b", 0), ("gr", 3), ("g2a", 1), ("g2b", 1), ("gr", 4),
-        ("g2a", 2), ("g2b", 2), ("g3", 0), ("g3", 1), ("g4", 0), ("gr", 5), ("g4", 1), ("g1", 3), ("g0", 6),
-        ("g3", 2), ("g1", 4), ("g0", 7), ("g4", 2), ("LQ", None), ("g1", 5), ("g0", 8), ("g2a", 3),
-        ("g2b", 3), ("A1", None), ("gr", 6), ("gr", 7), ("g2a", 4), ("g2b", 4),
+        ("g2a", 2), ("g2b", 2), ("g3", 0), ("g3", 1), ("g4", 0), ("g4", 1), ("gr", 5), ("g3", 2), ("g1", 3),
+        ("g0", 6), ("g4", 2), ("LQ", None), ("g1", 4), ("g0", 7), ("g1", 5), ("g0", 8), ("A1", None),
+        ("gr", 6), ("gr", 7), ("g2a", 3), ("g2b", 3), ("g2a", 4), ("g2b", 4),
     ],
     "H": [
         [
@@ -1277,21 +1277,21 @@
             ("g3", 3), ("g1", 7), ("g1", 8),
         ],
         [
-            ("g3", 4), ("g4", 3), ("LO", None), ("g3", 5),
-        ],
-        [
-            ("g4", 4), ("L", 0), ("g4", 5),
+            ("g3", 4), ("g4", 3), ("LO", None),
+        ],
+        [
+            ("g3", 5), ("g4", 4), ("L", 0),
         ],
     ],
     "A3": [
-        ("A3", None), ("L", 1), ("g2a", 6), ("g2b", 6),
+        ("A3", None), ("g2a", 6), ("g2b", 6), ("g4", 5), ("L", 1),
     ],
     "F": [
         [
             ("g2a", 7), ("g2b", 7),
         ],
         [
-            ("g3", 6), ("g2a", 8), ("g2b", 8),
+            ("g2a", 8), ("g2b", 8),
         ],
         [
             ("L", 4), ("c2a", 1), ("c2b", 1),
@@ -1308,7 +1308,7 @@
             ("z1", 0),
         ],
         [
-            ("g3", 7), ("c1", 1), ("g4", 6), ("L", 2), ("g4", 7), ("L", 3), ("g3", 8), ("g4", 8),
+            ("g3", 6), ("c1", 1), ("g3", 7), ("g4", 6), ("L", 2), ("g4", 7), ("L", 3), ("g3", 8), ("g4", 8),
         ],
         [
             ("c1", 2),
@@ -1321,32 +1321,30 @@
         ],
     ],
     "B1": [
-        ("B1", None), ("c4", 1), ("c2a", 3), ("c2b", 3), ("B2", None), ("c1", 5),
+        ("B1", None), ("c4", 1), ("c2a", 3), ("c2b", 3), ("B2", None), ("z3a", 0), ("z3b", 0), ("c1", 5),
     ],
     "K": [
         [
-            ("z3a", 0), ("z3b", 0),
-        ],
-        [
             ("c4", 2), ("c2a", 4), ("c2b", 4),
         ],
+        [],
         [
             ("c5a", 1), ("c5b", 1),
         ],
         [
-            ("c3", 3), ("c2a", 5), ("c2b", 5),
-        ],
-        [
-            ("z4", 0),
+            ("z4", 0), ("c3", 3), ("c2b", 5), ("c2a", 5),
+        ],
+        [
+            ("c5a", 2),
         ],
     ],
     "D1": [
-        ("D1", None), ("c5a", 2), ("c5b", 2), ("D3", None), ("c3", 4), ("c6", 1), ("c4", 3), ("D2", None),
-        ("c3", 5), ("c1", 6), ("D4", None), ("c5a", 0), ("c5b", 0), ("c6", 2), ("c1", 7), ("c1", 8),
-        ("c7", 1), ("c5a", 3), ("c5b", 3), ("c7", 2), ("c2b", 6), ("c2a", 6), ("c4", 4), ("c6", 0),
-        ("c2b", 7), ("c7", 0), ("c2a", 7), ("c4", 5), ("c2b", 8), ("c2a", 8), ("c6", 3), ("c7", 3), ("c3", 6),
-        ("c5a", 4), ("c5b", 4), ("c3", 7), ("c5a", 5), ("c5b", 5), ("c3", 8), ("c6", 4), ("c7", 4), ("c6", 5),
-        ("c4", 6), ("c7", 5), ("c4", 7), ("c5a", 6), ("c5b", 6), ("c4", 8), ("c6", 6), ("c5a", 7), ("c5b", 7),
+        ("D1", None), ("c5b", 2), ("D3", None), ("c6", 1), ("c3", 4), ("c4", 3), ("D2", None), ("c5a", 0),
+        ("c5b", 0), ("c1", 6), ("D4", None), ("c6", 2), ("c3", 5), ("c1", 7), ("c1", 8), ("c7", 1),
+        ("c5a", 3), ("c7", 2), ("c5b", 3), ("c6", 0), ("c7", 0), ("c2b", 6), ("c2a", 6), ("c4", 4),
+        ("c2b", 7), ("c2a", 7), ("c4", 5), ("c2b", 8), ("c2a", 8), ("c6", 3), ("c7", 3), ("c3", 6),
+        ("c5a", 4), ("c5b", 4), ("c3", 7), ("c5a", 5), ("c5b", 5), ("c3", 8), ("c6", 4), ("c6", 5), ("c4", 6),
+        ("c7", 4), ("c7", 5), ("c4", 7), ("c5a", 6), ("c5b", 6), ("c4", 8), ("c6", 6), ("c5a", 7), ("c5b", 7),
         ("c7", 6), ("c6", 7), ("c7", 7), ("c5a", 8), ("c5b", 8), ("c6", 8), ("c7", 8),
     ],
 }

time: 224 us -> 224 us (level)
  no operation moved by 1% of the time
where the time goes in v4:
time: 224 us
  Pallas kernels  220 us (98%)
  local copies, waits for them, and re-layouts  2.49 us (1%)
    pallas_call x1, Pallas kernels, layer(): pl.pallas_call(layer_kernel, name='layer', out_shape=[S((960, 512), bf16)...  192 us
    pallas_call x1, Pallas kernels, adam(): pl.pallas_call(adam_kernel, name='adam', grid=(8,), out_shape=shapes, in_...  27.6 us

profile of v4, /device:TPU:0, one launch (start us, length us, event | category | flops | bytes accessed | tf_op | source)
XLA Modules:
  0.0 223.8 jit_solution(9846709010320989017)
XLA Ops:
  0.7 0.5 fusion.2.freq
  1.2 192.4 %layer.1 = (bf16[960,512]{1,0:T(8,128)(2,1)}, bf16[960,512]{1,0:T(8,128)(2,1)}, bf16[8,2560,128]{2,1,0:T(8,128)(2,1)}, bf16[8,3,2560,128]{3,2,1,0:T(8,128)(2,1)}...) custom-call(bf16[960,512]{1,0:T(8,128)(2,1)} %bitcast.16, bf16[960,512]{1,0:T(8,128)(2,1)} %bitcast.17, ...), custom_call_target="tpu_custom_call" | custom-call | tf_op jit(solution)/shard_map/layer/pallas_call | solution.py:1231
  193.6 0.0 copy-start.1
  193.6 27.6 %adam.1 = (f32[2,240]{1,0:T(2,128)}, f32[240,1600]{1,0:T(8,128)}, f32[240,960]{1,0:T(8,128)}, f32[240,5120]{1,0:T(8,128)}, f32[960,640]{1,0:T(8,128)}, /*index=5...) custom-call(bf16[8,2560,128]{2,1,0:T(8,128)(2,1)} %get-tuple-element, ...), custom_call_target="tpu_custom_call" | custom-call | tf_op jit(solution)/shard_map/adam/pallas_call | solution.py:439
  221.3 0.0 copy-start
  221.3 0.0 copy-done.1
  221.3 0.9 copy.42
  222.2 0.6 copy-done
  222.8 0.9 copy.43
Async XLA Ops:
  193.6 27.7 %copy-start.1 = (bf16[960,512]{1,0:T(8,128)(2,1)S(1)}, bf16[960,512]{1,0:T(8,128)(2,1)}, u32[]{:S(2)}) copy-start(bf16[960,512]{1,0:T(8,128)(2,1)} %get-tuple-element.45) | copy-start | bytes 2949124
  221.3 1.6 copy-start
